TPU v7x, 256 devices: a whole 4x4x8 slice. The times are simulated.
256 devices in a mesh: gx: 16 (over z_hi, x), gy: 16 (over z_lo, y, core).
Axes of the slice: x: 4, y: 4, z: 8 (z_hi: 4, z_lo: 2; z = z_hi * 2 + z_lo), core: 2. Of those that a mesh axis runs over, the one named last changes fastest.
Arguments:
- features: bfloat16 [16, 16, 16, 48, 512], P('gx', 'gy'), may hold values from -6 to 6
- block_slots: int32 [16, 16, 16], P('gx', 'gy'), may hold values from 0 to 15, as said below
- block_count: int32 [16, 16], P('gx', 'gy'), may hold values from 2 to 16
- cotangent: bfloat16 [16, 16, 16, 48, 512], P('gx', 'gy'), may hold values from -6 to 6
- fine_weight: bfloat16 [48, 27, 48], replicated, may hold values from -0.15625 to 0.15625
- down_weight: bfloat16 [48, 8, 48], replicated, may hold values from -0.3125 to 0.3125
- coarse_weight: bfloat16 [48, 27, 48], replicated, may hold values from -0.15625 to 0.15625
- up_weight: bfloat16 [8, 48, 48], replicated, may hold values from -0.875 to 0.875
Outputs:
- output: bfloat16 [16, 16, 16, 48, 512], P('gx', 'gy')
- input_grad: bfloat16 [16, 16, 16, 48, 512], P('gx', 'gy')
- fine_weight_grad: float32 [48, 27, 48], replicated
- down_weight_grad: float32 [48, 8, 48], replicated
- coarse_weight_grad: float32 [48, 27, 48], replicated
- up_weight_grad: float32 [8, 48, 48], replicated
Inputs may be any that keep to these rules, and one draw needn't show every extreme that they name: `block_slots`: on each device the 16 entries are distinct, so every block position of the region appears once.
All inputs are finite; a program needn't handle non-finite values.
Results may differ from a plain program's by a relative error of at most 0.008.
Values may be sent and summed in bfloat16 or wider, within the bound.
A program may use at most 192 MiB of HBM per device.

v0:
```python
import math

import jax
import jax.numpy as jnp
from jax import lax
from jax.sharding import PartitionSpec as P

BLOCK = 8
VOX = 512
BX = 1
BY = 16


def with_halo(array, sides, width):
    for axis, dim in sides:
        devices, length = (lax.axis_size(axis), array.shape[dim])
        up = [(i, (i + 1) % devices) for i in range(devices - 1)]
        down = [(j, i) for i, j in up]
        last = lax.slice_in_dim(array, length - width, length, axis=dim)
        first = lax.slice_in_dim(array, 0, width, axis=dim)
        before = lax.ppermute(last, axis, up)
        after = lax.ppermute(first, axis, down)
        array = jnp.concatenate([before, array, after], axis=dim)
    return array


def split_parity(fine):
    lead = fine.shape[:-2]
    chans = fine.shape[-2]
    count = len(lead)
    shaped = fine.reshape(lead + (chans, 4, 2, 4, 2, 4, 2))
    order = tuple(range(count)) + (
        count + 2,
        count + 4,
        count + 6,
        count,
        count + 1,
        count + 3,
        count + 5,
    )
    return shaped.transpose(order).reshape(lead + (8, chans, 64))


def join_parity(parts):
    lead = parts.shape[:-3]
    chans = parts.shape[-2]
    count = len(lead)
    shaped = parts.reshape(lead + (2, 2, 2, chans, 4, 4, 4))
    order = tuple(range(count)) + (
        count + 3,
        count + 4,
        count,
        count + 5,
        count + 1,
        count + 6,
        count + 2,
    )
    return shaped.transpose(order).reshape(lead + (chans, 512))


def smooth_gate(value):
    return value * jax.nn.sigmoid(value)


def gate_slope(value):
    sigma = jax.nn.sigmoid(value)
    return sigma * (1.0 + value * (1.0 - sigma))


def block_grid(blocks, places, edge):
    chans = blocks.shape[1]
    dense = jnp.zeros((BX * BY, chans, edge**3), blocks.dtype).at[places].set(blocks)
    dense = dense.reshape(BX, BY, chans, edge, edge, edge)
    dense = dense.transpose(2, 3, 0, 4, 1, 5)
    return dense.reshape(chans, edge, BX * edge, BY * edge)


def grid_blocks(grid, places, edge):
    chans = grid.shape[0]
    shaped = grid.reshape(chans, edge, BX, edge, BY, edge).transpose(2, 4, 0, 1, 3, 5)
    return shaped.reshape(BX * BY, chans, edge**3)[places]


def depth_pad(grid):
    return jnp.pad(grid, ((0, 0), (1, 1), (0, 0), (0, 0)))


def conv_forward(padded, weight, edge):
    width_x = padded.shape[2] - 2
    width_y = padded.shape[3] - 2
    total = jnp.zeros((weight.shape[0], edge, width_x, width_y), jnp.float32)
    for depth in range(3):
        for across in range(3):
            for along in range(3):
                index = 9 * depth + 3 * across + along
                piece = padded[
                    :, depth : depth + edge, across : across + width_x, along : along + width_y
                ]
                total = total + jnp.einsum(
                    "oc,czxy->ozxy", weight[:, index, :], piece, preferred_element_type=jnp.float32
                )
    return total


def conv_backward(padded, weight, edge):
    width_x = padded.shape[2] - 2
    width_y = padded.shape[3] - 2
    total = jnp.zeros((weight.shape[2], edge, width_x, width_y), jnp.float32)
    for depth in range(3):
        for across in range(3):
            for along in range(3):
                index = 9 * depth + 3 * across + along
                piece = padded[
                    :,
                    2 - depth : 2 - depth + edge,
                    2 - across : 2 - across + width_x,
                    2 - along : 2 - along + width_y,
                ]
                total = total + jnp.einsum(
                    "oc,ozxy->czxy", weight[:, index, :], piece, preferred_element_type=jnp.float32
                )
    return total


def kernel_terms(grad_grid, padded, edge):
    width_x = padded.shape[2] - 2
    width_y = padded.shape[3] - 2
    terms = []
    for depth in range(3):
        for across in range(3):
            for along in range(3):
                piece = padded[
                    :, depth : depth + edge, across : across + width_x, along : along + width_y
                ]
                terms.append(
                    jnp.einsum(
                        "ozxy,czxy->oc", grad_grid, piece, preferred_element_type=jnp.float32
                    )
                )
    return jnp.stack(terms, axis=1)


def on_device(
    features,
    block_slots,
    block_count,
    cotangent,
    fine_weight,
    down_weight,
    coarse_weight,
    up_weight,
):
    slot_count = features.shape[2]
    chans = features.shape[3]
    half = BLOCK // 2
    places = block_slots.reshape(slot_count)
    live_count = block_count.reshape(())
    live = lax.iota(jnp.int32, slot_count) < live_count
    live_blocks = live[:, None, None]
    zero_half = jnp.zeros((), jnp.bfloat16)
    inputs = jnp.where(live_blocks, features.reshape(slot_count, chans, VOX), zero_half)
    grad_out = jnp.where(live_blocks, cotangent.reshape(slot_count, chans, VOX), zero_half)
    fine_pad = depth_pad(with_halo(block_grid(inputs, places, BLOCK), (("gx", 2), ("gy", 3)), 1))
    hidden_all = jnp.where(
        live_blocks, grid_blocks(conv_forward(fine_pad, fine_weight, BLOCK), places, BLOCK), 0.0
    )
    active_all = smooth_gate(hidden_all).astype(jnp.bfloat16)
    lowered_all = jnp.einsum(
        "oqc,sqcv->sov", down_weight, split_parity(active_all), preferred_element_type=jnp.float32
    )
    lowered_all = jnp.where(live_blocks, lowered_all, 0.0).astype(jnp.bfloat16)
    coarse_pad = depth_pad(
        with_halo(block_grid(lowered_all, places, half), (("gx", 2), ("gy", 3)), 1)
    )
    coarse = grid_blocks(conv_forward(coarse_pad, coarse_weight, half), places, half)
    rect = smooth_gate(coarse).astype(jnp.bfloat16)
    upward = join_parity(
        jnp.einsum("qoc,scv->sqov", up_weight, rect, preferred_element_type=jnp.float32)
    )
    output = jnp.where(live_blocks, hidden_all + upward, 0.0).astype(jnp.bfloat16)
    grad_parts = split_parity(grad_out)
    grad_rect = jnp.einsum(
        "qoc,sqov->scv", up_weight, grad_parts, preferred_element_type=jnp.float32
    )
    grad_coarse = jnp.where(live_blocks, grad_rect * gate_slope(coarse), 0.0).astype(jnp.bfloat16)
    up_local = jnp.einsum("sqov,scv->qoc", grad_parts, rect, preferred_element_type=jnp.float32)
    grad_coarse_grid = block_grid(grad_coarse, places, half)
    coarse_local = kernel_terms(grad_coarse_grid, coarse_pad, half)
    grad_coarse_pad = depth_pad(with_halo(grad_coarse_grid, (("gx", 2), ("gy", 3)), 1))
    grad_down = grid_blocks(conv_backward(grad_coarse_pad, coarse_weight, half), places, half)
    grad_down = jnp.where(live_blocks, grad_down, 0.0).astype(jnp.bfloat16)
    down_local = jnp.einsum(
        "sov,sqcv->oqc", grad_down, split_parity(active_all), preferred_element_type=jnp.float32
    )
    grad_act = join_parity(
        jnp.einsum("oqc,sov->sqcv", down_weight, grad_down, preferred_element_type=jnp.float32)
    )
    grad_hidden = grad_out.astype(jnp.float32) + grad_act * gate_slope(hidden_all)
    grad_hidden = jnp.where(live_blocks, grad_hidden, 0.0).astype(jnp.bfloat16)
    grad_hidden_grid = block_grid(grad_hidden, places, BLOCK)
    grad_hidden_pad = depth_pad(with_halo(grad_hidden_grid, (("gx", 2), ("gy", 3)), 1))
    fine_local = kernel_terms(grad_hidden_grid, fine_pad, BLOCK)
    input_grad = grid_blocks(conv_backward(grad_hidden_pad, fine_weight, BLOCK), places, BLOCK)
    input_grad = jnp.where(live_blocks, input_grad, 0.0).astype(jnp.bfloat16)
    fine_total, down_total, coarse_total, up_total = lax.psum(
        (fine_local, down_local, coarse_local, up_local), ("gx", "gy")
    )
    scale = 1.0 / math.sqrt(slot_count * VOX * lax.axis_size("gx") * lax.axis_size("gy"))
    shape_out = (1, 1, slot_count, chans, VOX)
    return (
        output.reshape(shape_out),
        input_grad.reshape(shape_out),
        fine_total * scale,
        down_total * scale,
        coarse_total * scale,
        up_total * scale,
    )


def solution(mesh):
    return jax.shard_map(
        on_device,
        mesh=mesh,
        in_specs=(
            P("gx", "gy", None, None, None),
            P("gx", "gy", None),
            P("gx", "gy"),
            P("gx", "gy", None, None, None),
            P(),
            P(),
            P(),
            P(),
        ),
        out_specs=(
            P("gx", "gy", None, None, None),
            P("gx", "gy", None, None, None),
            P(),
            P(),
            P(),
            P(),
        ),
        check_vma=False,
    )
```

profile of v0, /device:TPU:1, one launch (start us, length us, event | category | flops | bytes accessed | tf_op | source)
XLA Modules:
  0.0 589.3 jit_solution(3717136386121825845)
XLA Ops:
  16.8 3.9 collective-permute-start
  24.1 2.9 copy.893
  31.1 4.0 collective-permute-start.2
  82.2 6.5 %fusion.661 = (bf16[48,8,8,128]{3,0,2,1:T(8,128)(2,1)}, bf16[48,8,8,128]{3,0,2,1:T(8,128)(2,1)}, bf16[48,8,8,128]{3,0,2,1:T(8,128)(2,1)}, bf16[48,8,8,128]{3,0,2...) fusion(bf16[48,10,10,130]{3,0,2,1:T(8,128)(2,1)S(1)} %select_ma, ...), kind=kLoop, calls=%fused_computation.811 | loop fusion | bytes 28311552 | tf_op jit(solution)/shard_map/slice | solution.py:96
  88.7 3.1 fusion.662
  92.5 13.9 %bitcast_add_fusion.10 = f32[48,8,8,128]{3,0,2,1:T(8,128)} fusion(f32[8,8,128,48]{2,3,1,0:T(8,128)} %fusion.368, f32[8,8,128,48]{2,3,1,0:T(8,128)} %fusion.371, f32[8,8,128,48]{2,3,1,0:T(8,128)} %fusion.374, f32[8,8,128,48]{2,3,1,0:T(8,128)} %fusion.377, f32[8,8,128,48]{2,3,1,0:T(8,128)} %fusion.380, f32[8,8,128,48]{2,3,1,0:T(8,128)} %fusion.383, ...), kind=kOutput, calls=%fused_computation.59 | convolution fusion | flops 47972352 | bytes 43266048 | tf_op jit(solution)/shard_map/oc,czxy->ozxy/dot_general | solution.py:99
  106.3 3.8 copy.872
  110.1 4.7 copy.873
  118.3 3.8 copy.875
  122.1 3.3 fusion.16
  129.3 4.2 collective-permute-start.4
  135.2 3.2 collective-permute-done.5
  138.6 5.1 collective-permute-start.6
  147.3 4.4 collective-permute-done.7
  170.4 3.0 fusion.82
  180.1 5.3 collective-permute-start.8
  187.1 5.2 copy.890
  192.3 4.7 copy.891
  215.8 4.4 collective-permute-done.11
  231.1 5.2 copy.936
  236.3 4.7 copy.937
  278.3 6.3 %collective-permute-start.12 = (bf16[48,8,1,128]{3,0,2,1:T(8,128)(2,1)S(1)}, bf16[48,8,1,128]{3,0,2,1:T(8,128)(2,1)S(1)}, u32[]{:S(2)}, u32[]{:S(2)}) collective-permute-start(bf16[48,8,1,128]{3,0,2,1:T(8,128)(2,1)S(1)} %get-tuple-element.72), channel_id=1, source_target_pairs={{0,16},{16,32},{32,48},{48,64},{64,80},{80,96},{96,112},{112,128},... | collective-permute-start | bytes 294920 | tf_op jit(solution)/shard_map/ppermute | solution.py:21
  352.1 12.1 %bitcast_add_fusion = bf16[48,8,8,128]{3,0,2,1:T(8,128)(2,1)S(1)} fusion(f32[8,8,128,48]{2,3,1,0:T(8,128)} %fusion.154, f32[8,8,128,48]{2,3,1,0:T(8,128)} %fusion.156, f32[8,8,128,48]{2,3,1,0:T(8,128)} %fusion.158, f32[8,8,128,48]{2,3,1,0:T(8,128)} %fusion.160, f32[8,8,128,48]{2,3,1,0:T(8,128)} %fusion.162, f32[8,8,128,48]{2,3,1,0:T(8,128)} %fusion.164, ...), kind=kOutput, calls=%fused_computation.45 | convolution fusion | flops 48365568 | bytes 42479616 | tf_op jit(solution)/shard_map/oc,ozxy->czxy/dot_general | solution.py:119
  370.9 205.5 %all-reduce.7.cloned.1.call-done = (f32[48,27,48]{2,0,1:T(8,128)}, f32[48,8,48]{2,0,1:T(8,128)}, f32[48,27,48]{2,0,1:T(8,128)}, f32[8,48,48]{2,1,0:T(8,128)}) async-done(((f32[48,27,48]{2,0,1:T(8,128)}, f32[48,8,48]{2,0,1:T(8,128)}, f32[48,27,48]{2,0,1:T(8,128)}, f32[8,48,48]{2,1,0:T(8,128)}), (f32[48,27,48]{2,0,1:T(8,128)}, f32[48,8,48]{2,0,1:T(8,128)}, f32[48,27,48]{2,0,1:T(8,128)}, ...) | async-done | bytes 645136 | tf_op jit(solution)/shard_map/psum | solution.py:205
  (444 shorter events, 249.1 us)
Async XLA Ops:
  7.2 157.6 %copy-start = (bf16[8,48,48]{2,1,0:T(8,128)(2,1)S(1)}, bf16[8,48,48]{2,1,0:T(8,128)(2,1)}, u32[]{:S(2)}) copy-start(bf16[8,48,48]{2,1,0:T(8,128)(2,1)} %param.15) | copy-start | bytes 110596
  7.2 569.3 %all-reduce.7.cloned.1.call-start = ((), (), s32[]{:S(2)}) async-start(), calls=%async_computation | async-start | bytes 3440640 | tf_op jit(solution)/shard_map/psum | solution.py:205
  12.1 10.0 %copy-start.2 = (bf16[16,48,512]{1,2,0:T(8,128)(2,1)}, bf16[16,48,512]{1,2,0:T(8,128)(2,1)S(1)}, u32[]{:S(2)}) copy-start(bf16[16,48,512]{1,2,0:T(8,128)(2,1)S(1)} %copy.858) | copy-start | bytes 2359300
  14.1 8.0 %copy-start.21 = (bf16[48,27,48]{2,0,1:T(8,128)(2,1)S(1)}, bf16[48,27,48]{2,0,1:T(8,128)(2,1)}, u32[]{:S(2)}) copy-start(bf16[48,27,48]{2,0,1:T(8,128)(2,1)} %param.12) | copy-start | bytes 373252
  16.8 13.3 %collective-permute-start = (bf16[48,8,1,128]{3,0,2,1:T(8,128)(2,1)}, bf16[48,8,1,128]{3,0,2,1:T(8,128)(2,1)S(1)}, u32[]{:S(2)}, u32[]{:S(2)}) collective-permute-start(bf16[48,8,1,128]{3,0,2,1:T(8,128)(2,1)} %get-tuple-element.76), channel_id=1, source_target_pairs={{0,16},{16,32},{32,48},{48,64},{64,80},{80,96},{96,112},{112,128},... | collective-permute-start | bytes 294920 | tf_op jit(solution)/shard_map/ppermute | solution.py:21
  20.7 9.3 %collective-permute-start.1 = (bf16[48,8,1,128]{3,0,2,1:T(8,128)(2,1)}, bf16[48,8,1,128]{3,0,2,1:T(8,128)(2,1)S(1)}, u32[]{:S(2)}, u32[]{:S(2)}) collective-permute-start(bf16[48,8,1,128]{3,0,2,1:T(8,128)(2,1)} %get-tuple-element.77), channel_id=1, source_target_pairs={{16,0},{32,16},{48,32},{64,48},{80,64},{96,80},{112,96},{128,112},... | collective-permute-start | bytes 294920 | tf_op jit(solution)/shard_map/ppermute | solution.py:22
  31.1 9.8 %collective-permute-start.2 = (bf16[48,8,10,1]{0,1,3,2:T(8,128)(2,1)S(1)}, bf16[48,8,10,1]{0,1,3,2:T(8,128)(2,1)S(1)}, u32[]{:S(2)}, u32[]{:S(2)}) collective-permute-start(bf16[48,8,10,1]{0,1,3,2:T(8,128)(2,1)S(1)} %copy.863), channel_id=1, source_target_pairs={{0,1},{1,2},{2,3},{3,4},{4,5},{5,6},{6,7},{7,8},{8,9},{9,10},{10,1... | collective-permute-start | bytes 23048 | tf_op jit(solution)/shard_map/ppermute | solution.py:21
  35.7 5.8 collective-permute-start.3
  126.4 8.4 %copy-start.23 = (bf16[48,27,48]{2,0,1:T(8,128)(2,1)S(1)}, bf16[48,27,48]{2,0,1:T(8,128)(2,1)}, u32[]{:S(2)}) copy-start(bf16[48,27,48]{2,0,1:T(8,128)(2,1)} %param.14) | copy-start | bytes 373252
  129.3 5.9 %collective-permute-start.4 = (bf16[48,4,1,64]{3,0,2,1:T(8,128)(2,1)S(1)}, bf16[48,4,1,64]{3,0,2,1:T(8,128)(2,1)S(1)}, u32[]{:S(2)}, u32[]{:S(2)}) collective-permute-start(bf16[48,4,1,64]{3,0,2,1:T(8,128)(2,1)S(1)} %get-tuple-element.114), channel_id=1, source_target_pairs={{0,16},{16,32},{32,48},{48,64},{64,80},{80,96},{96,112},{112,128},... | collective-permute-start | bytes 73736 | tf_op jit(solution)/shard_map/ppermute | solution.py:21
  133.5 4.8 collective-permute-start.5
  138.6 8.7 %collective-permute-start.6 = (bf16[48,4,6,1]{3,0,2,1:T(8,128)(2,1)S(1)}, bf16[48,4,6,1]{3,0,2,1:T(8,128)(2,1)S(1)}, u32[]{:S(2)}, u32[]{:S(2)}) collective-permute-start(bf16[48,4,6,1]{3,0,2,1:T(8,128)(2,1)S(1)} %get-tuple-element.108), channel_id=1, source_target_pairs={{0,1},{1,2},{2,3},{3,4},{4,5},{5,6},{6,7},{7,8},{8,9},{9,10},{10,1... | collective-permute-start | bytes 6920 | tf_op jit(solution)/shard_map/ppermute | solution.py:21
  143.7 8.0 %collective-permute-start.7 = (bf16[48,4,6,1]{3,0,2,1:T(8,128)(2,1)S(1)}, bf16[48,4,6,1]{3,0,2,1:T(8,128)(2,1)S(1)}, u32[]{:S(2)}, u32[]{:S(2)}) collective-permute-start(bf16[48,4,6,1]{3,0,2,1:T(8,128)(2,1)S(1)} %get-tuple-element.109), channel_id=1, source_target_pairs={{1,0},{2,1},{3,2},{4,3},{5,4},{6,5},{7,6},{8,7},{9,8},{10,9},{11,1... | collective-permute-start | bytes 6920 | tf_op jit(solution)/shard_map/ppermute | solution.py:22
  169.1 10.7 %copy-start.16 = (bf16[48,4,1,4,16,4]{0,5,4,3,1,2:T(4,128)(2,1)}, bf16[48,4,1,4,16,4]{0,5,4,3,1,2:T(4,128)(2,1)S(1)}, u32[]{:S(2)}) copy-start(bf16[48,4,1,4,16,4]{0,5,4,3,1,2:T(4,128)(2,1)S(1)} %copy.898) | copy-start | bytes 294916
  180.1 29.8 %collective-permute-start.8 = (bf16[48,4,1,64]{3,0,2,1:T(8,128)(2,1)S(1)}, bf16[48,4,1,64]{3,0,2,1:T(8,128)(2,1)S(1)}, u32[]{:S(2)}, u32[]{:S(2)}) collective-permute-start(bf16[48,4,1,64]{3,0,2,1:T(8,128)(2,1)S(1)} %get-tuple-element.110), channel_id=1, source_target_pairs={{0,16},{16,32},{32,48},{48,64},{64,80},{80,96},{96,112},{112,128},... | collective-permute-start | bytes 73736 | tf_op jit(solution)/shard_map/ppermute | solution.py:21
  185.4 24.5 %collective-permute-start.9 = (bf16[48,4,1,64]{3,0,2,1:T(8,128)(2,1)S(1)}, bf16[48,4,1,64]{3,0,2,1:T(8,128)(2,1)S(1)}, u32[]{:S(2)}, u32[]{:S(2)}) collective-permute-start(bf16[48,4,1,64]{3,0,2,1:T(8,128)(2,1)S(1)} %get-tuple-element.111), channel_id=1, source_target_pairs={{16,0},{32,16},{48,32},{64,48},{80,64},{96,80},{112,96},{128,112},... | collective-permute-start | bytes 73736 | tf_op jit(solution)/shard_map/ppermute | solution.py:22
  206.5 8.0 %copy-start.24 = (bf16[48,27,48]{2,0,1:T(8,128)(2,1)S(1)}, bf16[48,27,48]{2,0,1:T(8,128)(2,1)}, u32[]{:S(2)}) copy-start(bf16[48,27,48]{2,0,1:T(8,128)(2,1)} %param.14) | copy-start | bytes 373252
  210.1 5.7 collective-permute-start.10
  212.2 8.0 %collective-permute-start.11 = (bf16[48,4,6,1]{3,0,2,1:T(8,128)(2,1)S(1)}, bf16[48,4,6,1]{3,0,2,1:T(8,128)(2,1)S(1)}, u32[]{:S(2)}, u32[]{:S(2)}) collective-permute-start(bf16[48,4,6,1]{3,0,2,1:T(8,128)(2,1)S(1)} %get-tuple-element.104), channel_id=1, source_target_pairs={{1,0},{2,1},{3,2},{4,3},{5,4},{6,5},{7,6},{8,7},{9,8},{10,9},{11,1... | collective-permute-start | bytes 6920 | tf_op jit(solution)/shard_map/ppermute | solution.py:22
  277.0 23.9 %collective-permute-start.13 = (bf16[48,8,1,128]{3,0,2,1:T(8,128)(2,1)}, bf16[48,8,1,128]{3,0,2,1:T(8,128)(2,1)S(1)}, u32[]{:S(2)}, u32[]{:S(2)}) collective-permute-start(bf16[48,8,1,128]{3,0,2,1:T(8,128)(2,1)} %get-tuple-element.73), channel_id=1, source_target_pairs={{16,0},{32,16},{48,32},{64,48},{80,64},{96,80},{112,96},{128,112},... | collective-permute-start | bytes 294920 | tf_op jit(solution)/shard_map/ppermute | solution.py:22
  278.3 22.7 %collective-permute-start.12 = (bf16[48,8,1,128]{3,0,2,1:T(8,128)(2,1)S(1)}, bf16[48,8,1,128]{3,0,2,1:T(8,128)(2,1)S(1)}, u32[]{:S(2)}, u32[]{:S(2)}) collective-permute-start(bf16[48,8,1,128]{3,0,2,1:T(8,128)(2,1)S(1)} %get-tuple-element.72), channel_id=1, source_target_pairs={{0,16},{16,32},{32,48},{48,64},{64,80},{80,96},{96,112},{112,128},... | collective-permute-start | bytes 294920 | tf_op jit(solution)/shard_map/ppermute | solution.py:21
  302.0 8.1 %collective-permute-start.14 = (bf16[48,8,10,1]{0,1,3,2:T(8,128)(2,1)S(1)}, bf16[48,8,10,1]{0,1,3,2:T(8,128)(2,1)S(1)}, u32[]{:S(2)}, u32[]{:S(2)}) collective-permute-start(bf16[48,8,10,1]{0,1,3,2:T(8,128)(2,1)S(1)} %copy.944), channel_id=1, source_target_pairs={{0,1},{1,2},{2,3},{3,4},{4,5},{5,6},{6,7},{7,8},{8,9},{9,10},{10,1... | collective-permute-start | bytes 23048 | tf_op jit(solution)/shard_map/ppermute | solution.py:21
  304.6 6.1 %collective-permute-start.15 = (bf16[48,8,10,1]{0,1,3,2:T(8,128)(2,1)S(1)}, bf16[48,8,10,1]{0,1,3,2:T(8,128)(2,1)S(1)}, u32[]{:S(2)}, u32[]{:S(2)}) collective-permute-start(bf16[48,8,10,1]{0,1,3,2:T(8,128)(2,1)S(1)} %copy.945), channel_id=1, source_target_pairs={{1,0},{2,1},{3,2},{4,3},{5,4},{6,5},{7,6},{8,7},{9,8},{10,9},{11,1... | collective-permute-start | bytes 23048 | tf_op jit(solution)/shard_map/ppermute | solution.py:22
  369.8 212.2 %copy-start.1 = (bf16[8,48,48]{2,1,0:T(8,128)(2,1)S(1)}, bf16[8,48,48]{2,1,0:T(8,128)(2,1)}, u32[]{:S(2)}) copy-start(bf16[8,48,48]{2,1,0:T(8,128)(2,1)} %param.15) | copy-start | bytes 110596
  (78 other events, 196.5 us)
Sparse Core Ops, SparseCore 0:
  301.1 275.3 all-reduce.6
where the time goes:
time: 598 us; the launch traced here: 589 us
  waiting for transfers between devices  219 us (37%)
  matrix products  176 us (29%)
  local copies, waits for them, and re-layouts  104 us (17%)
  starting transfers between devices  47.2 us (8%)
  other arithmetic  25.1 us (4%)
  between operations  16.8 us (3%)
    psum x1, waiting for transfers between devices, on_device(): lax.psum((fine_local, down_local, coarse_local, up_local), ('gx', 'gy'))  206 us
    dot_general x54, matrix products, conv_backward(): jnp.einsum('oc,ozxy->czxy', weight[:, index, :], piece, preferred_element...  62.7 us
    dot_general x54, matrix products, conv_forward(): jnp.einsum('oc,czxy->ozxy', weight[:, index, :], piece, preferred_element...  61.4 us
    dot_general x54, matrix products, kernel_terms(): jnp.einsum('ozxy,czxy->oc', grad_grid, piece, preferred_element_type=jnp....  39.8 us
    ppermute x8, starting transfers between devices, with_halo(): before = lax.ppermute(last, axis, up)  32.9 us
    ppermute x8, starting transfers between devices, with_halo(): after = lax.ppermute(first, axis, down)  14.2 us
    unnamed x173, local copies, waits for them, and re-layouts  13.5 us
    slice x4, local copies, waits for them, and re-layouts, conv_forward(): padded[:, depth:depth + edge, across:across + width_x, along:along + widt...  13.3 us
  transfers between devices with their start and end apart: 17, of which 6 were waited for; matrix products, arithmetic and copies ran while one was open for 20% of the time, Pallas kernels for 0%

commit v1 on v0

v1 whole, which is shorter than its diff:
```python
import math

import jax
import jax.numpy as jnp
from jax import lax
from jax.experimental import pallas as pl
from jax.experimental.pallas import tpu as pltpu
from jax.sharding import PartitionSpec as P

C = 48
SLOTS = 16
LANE = 128
NX = 16
NY = 16
ROWS = 1536
CHUNK = ROWS // NX
F32 = jnp.float32
BF16 = jnp.bfloat16
MESH = pl.DeviceIdType.MESH


def dot(a, b):
    return jnp.dot(a, b, preferred_element_type=F32)


def dot_t(a, b):
    return lax.dot_general(a, b, (((1,), (1,)), ((), ())), preferred_element_type=F32)


def iota(shape, dim):
    return lax.broadcasted_iota(jnp.int32, shape, dim)


def one_hot(cond):
    return jnp.where(cond, 1.0, 0.0).astype(BF16)


def build_shift(s_ref, count, last):
    row = iota((256, 256), 0)
    col = iota((256, 256), 1)
    lane = col % LANE
    right = col >= LANE
    if last == 127:
        before = jnp.where(lane < 64, lane + 63, lane - 64)
        after = jnp.where(lane < 64, lane + 64, lane - 63)
        before = jnp.where(lane == 0, -1, before)
        after = jnp.where(lane == 127, -1, after)
    else:
        before = jnp.where((lane == 0) | (lane > last), -1, lane - 1)
        after = jnp.where(lane >= last, -1, lane + 1)
    source = jnp.where(right, after, before)
    place = jnp.where(lane == jnp.where(right, last, 0), jnp.where(right, LANE + 8, LANE), -512)

    @pl.loop(0, count)
    def _(x):
        s_ref[x] = one_hot((row == source) | (row == place + x))


def build_edge(t_ref, length, last):
    row = iota((length, LANE), 0)
    col = iota((length, LANE), 1)
    lane = row % LANE
    x = row // LANE
    t_ref[...] = one_hot(((lane == last) & (col == x)) | ((lane == 0) & (col == x + 8)))


def build_places(e_ref, slots_ref, live_count):
    e_ref[...] = jnp.zeros_like(e_ref)
    row = iota((16, 256), 0)
    col = iota((16, 256), 1)
    y = row % 8
    own = (row // 8) == (col // LANE)
    spot = col % LANE - 64 * (y % 2) - y // 2

    @pl.loop(0, SLOTS)
    def _(s):
        place = jnp.where(s < live_count, slots_ref[0, s], 4096)
        tile = one_hot(own & (spot == 4 * place))
        for j in range(4):
            e_ref[pl.ds(pl.multiple_of(64 * s + 16 * j, 16), 16), 256 * j : 256 * j + 256] = tile


def live_lanes(slots_ref, live_count):
    spot = (iota((8, LANE), 1) % 64) // 4

    def step(s, total):
        place = jnp.where(s < live_count, slots_ref[0, s], 4096)
        return total + jnp.where(spot == place, 1.0, 0.0)

    return lax.fori_loop(0, SLOTS, step, jnp.zeros((8, LANE), F32))


def to_grid(blocks, work, e_ref, grid):
    @pl.loop(0, 8)
    def _(t):
        lanes = pl.ds(pl.multiple_of(t * LANE, LANE), LANE)
        for pair in range(4):
            one = blocks[2 * t, :, pair * LANE : (pair + 1) * LANE]
            two = blocks[2 * t + 1, :, pair * LANE : (pair + 1) * LANE]
            work[2 * pair, :, lanes] = jnp.concatenate([one[:, :64], two[:, :64]], axis=1)
            work[2 * pair + 1, :, lanes] = jnp.concatenate([one[:, 64:], two[:, 64:]], axis=1)

    @pl.loop(0, 4)
    def _(n):
        lanes = pl.ds(pl.multiple_of(n * 256, 256), 256)
        moved = dot(work[...].reshape(8 * C, 1024), e_ref[:, lanes])
        grid[:, :, lanes] = moved.astype(BF16).reshape(8, C, 256)


def to_blocks(grid, e_ref, blocks):
    @pl.loop(0, 4)
    def _(n):
        rows = pl.ds(pl.multiple_of(n * 256, 256), 256)
        moved = dot_t(grid[...].reshape(8 * C, 1024), e_ref[rows, :])
        moved = moved.astype(BF16).reshape(8, C, 256)
        for pair in range(4):
            for k in range(4):
                low = moved[2 * pair, :, 64 * k : 64 * k + 64]
                high = moved[2 * pair + 1, :, 64 * k : 64 * k + 64]
                blocks[4 * n + k, :, pair * LANE : (pair + 1) * LANE] = jnp.concatenate(
                    [low, high], axis=1
                )


def pack_edges(grid, depth, t_ref, packed):
    edges = dot(grid.reshape(depth * C, grid.shape[2]), t_ref[...]).reshape(depth, C, LANE)
    total = edges[0]
    for z in range(1, depth):
        total = total + pltpu.roll(edges[z], 16 * z, 1)
    packed[...] = total.astype(BF16)


def unpack_edges(received, row, left_ok, right_ok, depth):
    lane = iota((C, LANE), 1) % 16
    left = jnp.where(left_ok, received[2 * row].astype(F32), 0.0)
    right = jnp.where(right_ok, received[2 * row + 1].astype(F32), 0.0)
    both = jnp.where(lane < 8, left, right)
    parts = [both] + [pltpu.roll(both, LANE - 16 * z, 1) for z in range(1, depth)]
    return jnp.stack(parts, axis=0).astype(BF16).reshape(depth * C, LANE)


def widen(grid, sides, received, s_ref, wide, count, depth, place):
    gx, gy = place
    low_ok, high_ok = gx > 0, gx < NX - 1
    left_ok, right_ok = gy > 0, gy < NY - 1

    def put(rows, halo, x, lanes):
        moved = dot(jnp.concatenate([rows, halo], axis=1), s_ref[x]).astype(BF16)
        wide[:, 0:C, lanes] = moved[:, :LANE].reshape(depth, C, LANE)
        wide[:, C : 2 * C, lanes] = rows.reshape(depth, C, LANE)
        wide[:, 2 * C : 3 * C, lanes] = moved[:, LANE:].reshape(depth, C, LANE)

    zero = jnp.zeros((depth * C, LANE), BF16)
    halo = unpack_edges(received, 0, left_ok & low_ok, right_ok & low_ok, depth)
    rows = jnp.where(low_ok, sides[0].reshape(depth * C, LANE), zero)
    put(rows, halo, count - 1, pl.ds(0, LANE))
    halo = unpack_edges(received, 2, left_ok & high_ok, right_ok & high_ok, depth)
    rows = jnp.where(high_ok, sides[1].reshape(depth * C, LANE), zero)
    put(rows, halo, 0, pl.ds((count + 1) * LANE, LANE))
    halo = unpack_edges(received, 1, left_ok, right_ok, depth)

    @pl.loop(0, count)
    def _(x):
        rows = grid[:, :, pl.ds(pl.multiple_of(x * LANE, LANE), LANE)].reshape(depth * C, LANE)
        put(rows, halo, x, pl.ds(pl.multiple_of((x + 1) * LANE, LANE), LANE))


def window(wide, z, first):
    return jnp.concatenate(
        [wide[z, :, pl.ds(pl.multiple_of(first + dx * LANE, LANE), 256)] for dx in range(3)], axis=0
    )


def convolve(wide, weight, total, depth, width):
    total[...] = jnp.zeros_like(total)

    @pl.loop(0, depth)
    def _(z):
        @pl.loop(0, width // 256)
        def _(n):
            first = pl.multiple_of(n * 256, 256)
            piece = dot(weight[...], window(wide, z, first)).reshape(3, C, 256)
            lanes = pl.ds(first, 256)
            total[pl.ds(z, 3), :, lanes] = total[pl.ds(z, 3), :, lanes] + piece


def kernel_terms(grad, wide, total, depth, width):
    total[...] = jnp.zeros_like(total)

    @pl.loop(0, depth)
    def _(z):
        @pl.loop(0, width // 256)
        def _(n):
            first = pl.multiple_of(n * 256, 256)
            lanes = pl.ds(first, 256)
            ahead = grad[pl.ds(z, 3), :, lanes].reshape(3 * C, 256)
            total[...] = total[...] + dot_t(ahead, window(wide, z, first))


def quarters(grid, wz):
    columns = []
    for a in range(2):
        for b in range(2):
            columns.append(
                jnp.concatenate(
                    [
                        grid[2 * wz + a, :, (2 * wx + b) * LANE : (2 * wx + b + 1) * LANE]
                        for wx in range(4)
                    ],
                    axis=1,
                )
            )
    return jnp.concatenate(columns, axis=0)


def tile_lanes(mask, rows, width):
    return jnp.broadcast_to(jnp.concatenate([mask] * (width // LANE), axis=1)[0:1], (rows, width))


def roll_half(value):
    parts = [
        pltpu.roll(value[:, k * LANE : (k + 1) * LANE], 64, 1) for k in range(value.shape[1] // LANE)
    ]
    return jnp.concatenate(parts, axis=1)


def slope(value):
    sigma = jax.nn.sigmoid(value)
    return sigma * (1.0 + value * (1.0 - sigma))


def section(
    slots_ref,
    count_ref,
    feat_hbm,
    cot_hbm,
    wf,
    wfb,
    wc,
    wcb,
    ddn,
    dga,
    uup,
    ugr,
    out_hbm,
    ig_hbm,
    gf_out,
    gc_out,
    gu_out,
    gd_out,
    feat,
    cot_in,
    work,
    places,
    shift_f,
    shift_c,
    edge_f,
    edge_c,
    fine,
    cot,
    fine3,
    hidden,
    act,
    low,
    low3,
    coarse,
    grect,
    rect2,
    gcoarse,
    gcoarse3,
    gdown2,
    ghid,
    ghid3,
    result,
    blocks_out,
    blocks_ig,
    term_f,
    term_c,
    term_u,
    term_d,
    packed,
    sides_f,
    sides_c,
    edges_in,
    grads,
    first_in,
    chunk,
    second_in,
    done,
    local_sem,
    send_sem,
    recv_sem,
    sum_send,
    sum_recv,
):
    gx = lax.axis_index("gx")
    gy = lax.axis_index("gy")
    here = (gx, gy)

    load_feat = pltpu.make_async_copy(feat_hbm, feat, local_sem.at[0])
    load_cot = pltpu.make_async_copy(cot_hbm, cot_in, local_sem.at[1])
    load_feat.start()
    load_cot.start()

    barrier = pltpu.get_barrier_semaphore()

    @pl.loop(1, NX)
    def _(d):
        pl.semaphore_signal(
            barrier, inc=1, device_id=(lax.rem(gx + d, NX), gy), device_id_type=MESH
        )
        pl.semaphore_signal(
            barrier, inc=1, device_id=(gx, lax.rem(gy + d, NY)), device_id_type=MESH
        )

    for dx in (1, NX - 1):
        for dy in (1, NY - 1):
            pl.semaphore_signal(
                barrier,
                inc=1,
                device_id=(lax.rem(gx + dx, NX), lax.rem(gy + dy, NY)),
                device_id_type=MESH,
            )

    live_count = count_ref[0, 0]
    build_places(places, slots_ref, live_count)
    build_shift(shift_f, 8, 127)
    build_shift(shift_c, 4, 63)
    build_edge(edge_f, 1024, 127)
    build_edge(edge_c, 512, 63)
    live = live_lanes(slots_ref, live_count)
    half_live = jnp.where(iota((8, LANE), 1) < 64, live, 0.0)
    lower = jnp.where(iota((8, LANE), 1) < 64, 1.0, 0.0)

    def exchange(step, source, depth, count, sides):
        copies = []
        for side in range(2):
            x = count - 1 if side == 0 else 0
            shift = 1 if side == 0 else NX - 1
            copies.append(
                pltpu.make_async_remote_copy(
                    src_ref=source.at[:, :, pl.ds(x * LANE, LANE)],
                    dst_ref=sides.at[side],
                    send_sem=send_sem.at[step, side],
                    recv_sem=recv_sem.at[step, side],
                    device_id=(lax.rem(gx + shift, NX), gy),
                    device_id_type=MESH,
                )
            )
        for row in range(3):
            for side in range(2):
                copies.append(
                    pltpu.make_async_remote_copy(
                        src_ref=packed.at[step],
                        dst_ref=edges_in.at[step, 2 * row + side],
                        send_sem=send_sem.at[step, 2 + 2 * row + side],
                        recv_sem=recv_sem.at[step, 2 + 2 * row + side],
                        device_id=(
                            lax.rem(gx + NX + 1 - row, NX),
                            lax.rem(gy + (1 if side == 0 else NY - 1), NY),
                        ),
                        device_id_type=MESH,
                    )
                )
        for copy in copies:
            copy.start()
        return copies

    load_feat.wait()
    to_grid(feat, work, places, fine)
    pack_edges(fine[...], 8, edge_f, packed.at[0])
    pl.semaphore_wait(barrier, 2 * (NX - 1) + 4)
    copies = exchange(0, fine, 8, 8, sides_f.at[0])

    load_cot.wait()
    to_grid(cot_in, work, places, cot)
    for wz in range(4):
        both = dot(ugr[...], quarters(cot, wz))
        grect[wz] = both[:C] + roll_half(both[C:])

    for copy in copies:
        copy.wait()
    widen(fine, sides_f.at[0], edges_in.at[0], shift_f, fine3, 8, 8, here)
    convolve(fine3, wf, hidden, 8, 1024)

    live_fine = tile_lanes(live, C, 1024)

    @pl.loop(0, 8)
    def _(z):
        value = hidden[z + 1] * live_fine
        hidden[z + 1] = value
        act[z] = (value * jax.nn.sigmoid(value)).astype(BF16)

    lower_mask = tile_lanes(lower, C, 512)
    for wz in range(4):
        both = dot(ddn[...], quarters(act, wz))
        low[wz] = ((both[:C] + roll_half(both[C:])) * lower_mask).astype(BF16)

    pack_edges(low[...], 4, edge_c, packed.at[1])
    copies = exchange(1, low, 4, 4, sides_c.at[0])
    for copy in copies:
        copy.wait()
    widen(low, sides_c.at[0], edges_in.at[1], shift_c, low3, 4, 4, here)
    convolve(low3, wc, coarse, 4, 512)

    gcoarse[...] = jnp.zeros_like(gcoarse)
    for wz in range(4):
        value = coarse[wz + 1]
        rect = value * jax.nn.sigmoid(value) * lower_mask
        rect2[wz, 0:C] = rect.astype(BF16)
        rect2[wz, C : 2 * C] = roll_half(rect).astype(BF16)
        gcoarse[wz + 1] = (grect[wz] * slope(value) * lower_mask).astype(BF16)

    pack_edges(gcoarse[1:5], 4, edge_c, packed.at[2])
    copies = exchange(2, gcoarse.at[pl.ds(1, 4)], 4, 4, sides_c.at[1])

    for wz in range(4):
        upward = dot(uup[...], rect2[wz])
        for a in range(2):
            for b in range(2):
                k = 2 * a + b
                for wx in range(4):
                    lanes = pl.ds((2 * wx + b) * LANE, LANE)
                    piece = upward[k * C : (k + 1) * C, wx * LANE : (wx + 1) * LANE]
                    result[2 * wz + a, :, lanes] = (
                        hidden[2 * wz + a + 1, :, lanes] + piece
                    ).astype(BF16)
    to_blocks(result, places, blocks_out)
    store_out = pltpu.make_async_copy(blocks_out, out_hbm, local_sem.at[2])
    store_out.start()
    kernel_terms(gcoarse, low3, term_c, 4, 512)
    total = jnp.zeros((4 * C, 2 * C), F32)
    for wz in range(4):
        total = total + dot_t(quarters(cot, wz), rect2[wz])
    term_u[...] = total

    for copy in copies:
        copy.wait()
    widen(gcoarse.at[pl.ds(1, 4)], sides_c.at[1], edges_in.at[2], shift_c, gcoarse3, 4, 4, here)
    convolve(gcoarse3, wcb, coarse, 4, 512)

    live_coarse = tile_lanes(half_live, C, 512)
    ghid[0] = jnp.zeros((C, 1024), BF16)
    ghid[9] = jnp.zeros((C, 1024), BF16)
    for wz in range(4):
        value = coarse[wz + 1] * live_coarse
        gdown2[wz, 0:C] = value.astype(BF16)
        gdown2[wz, C : 2 * C] = roll_half(value).astype(BF16)
        back = dot(dga[...], gdown2[wz])
        for a in range(2):
            for b in range(2):
                k = 2 * a + b
                for wx in range(4):
                    lanes = pl.ds((2 * wx + b) * LANE, LANE)
                    piece = back[k * C : (k + 1) * C, wx * LANE : (wx + 1) * LANE]
                    ghid[2 * wz + a + 1, :, lanes] = (
                        cot[2 * wz + a, :, lanes].astype(F32)
                        + piece * slope(hidden[2 * wz + a + 1, :, lanes])
                    ).astype(BF16)

    pack_edges(ghid[1:9], 8, edge_f, packed.at[3])
    copies = exchange(3, ghid.at[pl.ds(1, 8)], 8, 8, sides_f.at[1])

    total = jnp.zeros((2 * C, 4 * C), F32)
    for wz in range(4):
        total = total + dot_t(gdown2[wz], quarters(act, wz))
    term_d[...] = total
    kernel_terms(ghid, fine3, term_f, 8, 1024)

    grads[...] = jnp.zeros_like(grads)
    for k in range(4):
        wide = min(LANE, 432 - k * LANE)
        lanes = slice(k * LANE, k * LANE + wide)
        grads[144 * k : 144 * k + 144, 0:wide] = term_f[:, lanes].astype(BF16)
        grads[576 + 144 * k : 720 + 144 * k, 0:wide] = term_c[:, lanes].astype(BF16)
    grads[1152:1344, 0:96] = term_u[...].astype(BF16)
    grads[1344:1440, :] = term_d[:, 0:LANE].astype(BF16)
    grads[1440:1536, 0:64] = term_d[:, LANE:192].astype(BF16)

    def chunk_rows(index):
        return pl.ds(pl.multiple_of(index * CHUNK, CHUNK), CHUNK)

    def first_copy(d):
        peer = lax.rem(gx + d, NX)
        return pltpu.make_async_remote_copy(
            src_ref=grads.at[chunk_rows(peer)],
            dst_ref=first_in.at[d],
            send_sem=sum_send.at[0, d],
            recv_sem=sum_recv.at[0, d],
            device_id=(peer, gy),
            device_id_type=MESH,
        )

    def second_copy(d):
        return pltpu.make_async_remote_copy(
            src_ref=chunk.at[0],
            dst_ref=second_in.at[d],
            send_sem=sum_send.at[1, d],
            recv_sem=sum_recv.at[1, d],
            device_id=(gx, lax.rem(gy + d, NY)),
            device_id_type=MESH,
        )

    def third_copy(d):
        return pltpu.make_async_remote_copy(
            src_ref=chunk.at[1],
            dst_ref=done.at[chunk_rows(gx)],
            send_sem=sum_send.at[2, d],
            recv_sem=sum_recv.at[2, d],
            device_id=(lax.rem(gx + d, NX), gy),
            device_id_type=MESH,
        )

    @pl.loop(1, NX)
    def _(d):
        first_copy(d).start()

    for copy in copies:
        copy.wait()
    widen(ghid.at[pl.ds(1, 8)], sides_f.at[1], edges_in.at[3], shift_f, ghid3, 8, 8, here)
    convolve(ghid3, wfb, hidden, 8, 1024)

    @pl.loop(1, NX)
    def _(d):
        first_copy(d).wait()

    own = grads[chunk_rows(gx), :].astype(F32)
    own = lax.fori_loop(1, NX, lambda d, acc: acc + first_in[d].astype(F32), own)
    chunk[0] = own.astype(BF16)

    @pl.loop(1, NY)
    def _(d):
        second_copy(d).start()

    @pl.loop(0, 8)
    def _(z):
        result[z] = hidden[z + 1].astype(BF16)

    to_blocks(result, places, blocks_ig)
    store_ig = pltpu.make_async_copy(blocks_ig, ig_hbm, local_sem.at[3])
    store_ig.start()

    @pl.loop(1, NY)
    def _(d):
        second_copy(d).wait()

    own = lax.fori_loop(1, NY, lambda d, acc: acc + second_in[d].astype(F32), own)
    chunk[1] = own.astype(BF16)

    @pl.loop(1, NX)
    def _(d):
        third_copy(d).start()

    done[chunk_rows(gx), :] = chunk[1]

    @pl.loop(1, NX)
    def _(d):
        third_copy(d).wait()

    scale = 1.0 / math.sqrt(SLOTS * 512 * NX * NY)
    for k in range(4):
        wide = min(LANE, 432 - k * LANE)
        lanes = slice(k * LANE, k * LANE + wide)
        gf_out[:, lanes] = done[144 * k : 144 * k + 144, 0:wide].astype(F32) * scale
        gc_out[:, lanes] = done[576 + 144 * k : 720 + 144 * k, 0:wide].astype(F32) * scale
    gu_out[...] = done[1152:1344, 0:96].astype(F32) * scale
    gd_out[:, 0:LANE] = done[1344:1440, :].astype(F32) * scale
    gd_out[:, LANE:192] = done[1440:1536, 0:64].astype(F32) * scale
    store_out.wait()
    store_ig.wait()


def on_device(
    features, block_slots, block_count, cotangent, fine_weight, down_weight, coarse_weight, up_weight
):
    def forward_rows(weight):
        return (
            weight.reshape(C, 3, 9, C)[:, ::-1].transpose(1, 0, 2, 3).reshape(3 * C, 9 * C)
        )

    def backward_rows(weight):
        return weight.reshape(C, 3, 9, C)[:, :, ::-1].transpose(1, 3, 2, 0).reshape(3 * C, 9 * C)

    down = down_weight.reshape(C, 4, 2, C)
    ddn = down.transpose(2, 0, 1, 3).reshape(2 * C, 4 * C)
    dga = down.transpose(1, 3, 2, 0).reshape(4 * C, 2 * C)
    up = up_weight.reshape(4, 2, C, C)
    uup = up.transpose(0, 2, 1, 3).reshape(4 * C, 2 * C)
    ugr = up.transpose(1, 3, 0, 2).reshape(2 * C, 4 * C)

    vmem = pl.BlockSpec(memory_space=pltpu.VMEM)
    smem = pl.BlockSpec(memory_space=pltpu.SMEM)
    anywhere = pl.BlockSpec(memory_space=pl.ANY)
    blocks = (SLOTS, C, 512)
    out, ig, gf, gc, gu, gd = pl.pallas_call(
        section,
        out_shape=(
            jax.ShapeDtypeStruct(blocks, BF16),
            jax.ShapeDtypeStruct(blocks, BF16),
            jax.ShapeDtypeStruct((3 * C, 9 * C), F32),
            jax.ShapeDtypeStruct((3 * C, 9 * C), F32),
            jax.ShapeDtypeStruct((4 * C, 2 * C), F32),
            jax.ShapeDtypeStruct((2 * C, 4 * C), F32),
        ),
        in_specs=[smem, smem, anywhere, anywhere] + [vmem] * 8,
        out_specs=(anywhere, anywhere, vmem, vmem, vmem, vmem),
        scratch_shapes=[
            pltpu.VMEM(blocks, BF16),
            pltpu.VMEM(blocks, BF16),
            pltpu.VMEM((8, C, 1024), BF16),
            pltpu.VMEM((1024, 1024), BF16),
            pltpu.VMEM((8, 256, 256), BF16),
            pltpu.VMEM((4, 256, 256), BF16),
            pltpu.VMEM((1024, LANE), BF16),
            pltpu.VMEM((512, LANE), BF16),
            pltpu.VMEM((8, C, 1024), BF16),
            pltpu.VMEM((8, C, 1024), BF16),
            pltpu.VMEM((8, 3 * C, 1280), BF16),
            pltpu.VMEM((10, C, 1024), F32),
            pltpu.VMEM((8, C, 1024), BF16),
            pltpu.VMEM((4, C, 512), BF16),
            pltpu.VMEM((4, 3 * C, 768), BF16),
            pltpu.VMEM((6, C, 512), F32),
            pltpu.VMEM((4, C, 512), F32),
            pltpu.VMEM((4, 2 * C, 512), BF16),
            pltpu.VMEM((6, C, 512), BF16),
            pltpu.VMEM((4, 3 * C, 768), BF16),
            pltpu.VMEM((4, 2 * C, 512), BF16),
            pltpu.VMEM((10, C, 1024), BF16),
            pltpu.VMEM((8, 3 * C, 1280), BF16),
            pltpu.VMEM((8, C, 1024), BF16),
            pltpu.VMEM(blocks, BF16),
            pltpu.VMEM(blocks, BF16),
            pltpu.VMEM((3 * C, 9 * C), F32),
            pltpu.VMEM((3 * C, 9 * C), F32),
            pltpu.VMEM((4 * C, 2 * C), F32),
            pltpu.VMEM((2 * C, 4 * C), F32),
            pltpu.VMEM((4, C, LANE), BF16),
            pltpu.VMEM((2, 2, 8, C, LANE), BF16),
            pltpu.VMEM((2, 2, 4, C, LANE), BF16),
            pltpu.VMEM((4, 6, C, LANE), BF16),
            pltpu.VMEM((ROWS, LANE), BF16),
            pltpu.VMEM((NX, CHUNK, LANE), BF16),
            pltpu.VMEM((2, CHUNK, LANE), BF16),
            pltpu.VMEM((NY, CHUNK, LANE), BF16),
            pltpu.VMEM((ROWS, LANE), BF16),
            pltpu.SemaphoreType.DMA((4,)),
            pltpu.SemaphoreType.DMA((4, 8)),
            pltpu.SemaphoreType.DMA((4, 8)),
            pltpu.SemaphoreType.DMA((3, NX)),
            pltpu.SemaphoreType.DMA((3, NX)),
        ],
        compiler_params=pltpu.CompilerParams(
            collective_id=0, has_side_effects=True, vmem_limit_bytes=50 * 1024 * 1024
        ),
        name="section",
    )(
        block_slots.reshape(1, SLOTS),
        block_count.reshape(1, 1),
        features.reshape(blocks),
        cotangent.reshape(blocks),
        forward_rows(fine_weight),
        backward_rows(fine_weight),
        forward_rows(coarse_weight),
        backward_rows(coarse_weight),
        ddn,
        dga,
        uup,
        ugr,
    )

    def kernel_grad(rows):
        return rows.reshape(3, C, 9, C)[::-1].transpose(1, 0, 2, 3).reshape(C, 27, C)

    shape_out = (1, 1) + blocks
    return (
        out.reshape(shape_out),
        ig.reshape(shape_out),
        kernel_grad(gf),
        gd.reshape(2, C, 4, C).transpose(1, 2, 0, 3).reshape(C, 8, C),
        kernel_grad(gc),
        gu.reshape(4, C, 2, C).transpose(0, 2, 1, 3).reshape(8, C, C),
    )


def solution(mesh):
    split = P("gx", "gy", None, None, None)
    return jax.shard_map(
        on_device,
        mesh=mesh,
        in_specs=(split, P("gx", "gy", None), P("gx", "gy"), split, P(), P(), P(), P()),
        out_specs=(split, split, P(), P(), P(), P()),
        check_vma=False,
    )
```

time: 598 us -> 123 us (0.21); the launches traced: 589 us -> 121 us
  waiting for transfers between devices: 219 us -> 0 us
  matrix products: 176 us -> 0 us
  Pallas kernels: 0 us -> 89.9 us
  local copies, waits for them, and re-layouts: 104 us -> 29.4 us
  starting transfers between devices: 47.2 us -> 0 us
  other arithmetic: 25.1 us -> 0 us
  between operations: 16.8 us -> 1.57 us
    psum x1 -> x0, waiting for transfers between devices: 206 us -> none  [on_device(): lax.psum((fine_local, down_local, coarse_local, up_local), ('gx', 'gy'))]
    dot_general x168 -> x0, matrix products: 176 us -> none  [the longest x54 62.7 us: conv_backward(): jnp.einsum('oc,ozxy->czxy', weight[:, index, :], piece, preferred_element...]
    pallas_call x0 -> x1, Pallas kernels: none -> 89.9 us  [on_device(): pl.pallas_call(section, out_shape=(jax.ShapeDtypeStruct(blocks, BF16), ja...]
    ppermute x16 -> x0, starting transfers between devices: 47.2 us -> none  [the longest x8 32.9 us: with_halo(): before = lax.ppermute(last, axis, up)]
    transpose x14 -> x6, local copies, waits for them, and re-layouts: 33.4 us -> 4.07 us  [the longest x2 2.22 us: kernel_grad(): rows.reshape(3, C, 9, C)[::-1].transpose(1, 0, 2, 3).reshape(C, 27, C)]
    slice x16 -> x0, local copies, waits for them, and re-layouts: 17.9 us -> none  [the longest x4 13.3 us: conv_forward(): padded[:, depth:depth + edge, across:across + width_x, along:along + widt...]
    ppermute x16 -> x0, waiting for transfers between devices: 13.9 us -> none  [the longest x8 12 us: with_halo(): after = lax.ppermute(first, axis, down)]
    concatenate x14 -> x0, other arithmetic: 9.59 us -> none  [with_halo(): array = jnp.concatenate([before, array, after], axis=dim)]
  transfers between devices with their start and end apart: 17 -> 0, of which waited for: 6 -> 0; matrix products, arithmetic and copies ran while one was open for 20% -> 0% of each run, Pallas kernels for 0% -> 0%
where the time goes in v1:
time: 123 us; the launch traced here: 121 us
  Pallas kernels  89.9 us (73%)
  local copies, waits for them, and re-layouts  29.4 us (24%)
  between operations  1.57 us (1%)
    pallas_call x1, Pallas kernels, on_device(): pl.pallas_call(section, out_shape=(jax.ShapeDtypeStruct(blocks, BF16), ja...  89.9 us
    unnamed x30, local copies, waits for them, and re-layouts  9.4 us
    rev x2, local copies, waits for them, and re-layouts, kernel_grad(): rows.reshape(3, C, 9, C)[::-1].transpose(1, 0, 2, 3).reshape(C, 27, C)  4.4 us
    rev x2, local copies, waits for them, and re-layouts, forward_rows(): weight.reshape(C, 3, 9, C)[:, ::-1].transpose(1, 0, 2, 3)  2.71 us
    reshape x8, local copies, waits for them, and re-layouts, forward_rows(): weight.reshape(C, 3, 9, C)[:, ::-1].transpose(1, 0, 2, 3)  2.5 us

profile of v1, /device:TPU:1, one launch (start us, length us, event | category | flops | bytes accessed | tf_op | source)
XLA Modules:
  0.0 120.9 jit_solution(12333067843188812019)
XLA Ops:
  0.6 1.2 %copy.42 = bf16[48,3,9,48]{0,1,3,2:T(4,128)(2,1)S(1)} copy(bf16[48,3,9,48]{3,0,2,1:T(8,128)(2,1)} %bitcast.51) | data formatting | bytes 248832 | tf_op jit(solution)/shard_map/reshape | solution.py:578
  1.9 1.4 %rev.18 = bf16[48,3,9,48]{0,1,3,2:T(4,128)(2,1)S(1)} reverse(bf16[48,3,9,48]{0,1,3,2:T(4,128)(2,1)S(1)} %copy.42), dimensions={1} | reverse | bytes 248832 | tf_op jit(solution)/shard_map/rev | solution.py:578
  3.6 0.9 copy-done.10
  5.1 0.9 copy-done.11
  6.3 1.4 %rev.20 = bf16[48,3,9,48]{0,1,3,2:T(4,128)(2,1)S(1)} reverse(bf16[48,3,9,48]{0,1,3,2:T(4,128)(2,1)S(1)} %copy.44), dimensions={1} | reverse | bytes 248832 | tf_op jit(solution)/shard_map/rev | solution.py:578
  8.7 0.7 copy-done.13
  9.6 0.7 reshape.100.dga
  10.4 0.7 reshape.102.uup
  11.3 0.7 reshape.103.ugr
  12.0 0.7 reshape.99.ddn
  14.1 0.8 copy-done.1
  14.9 0.8 copy-done.2
  15.7 0.8 copy-done.3
  16.5 0.8 copy-done.4
  17.3 89.9 %section.1 = (bf16[16,48,512]{2,1,0:T(8,128)(2,1)S(1)}, bf16[16,48,512]{2,1,0:T(8,128)(2,1)S(1)}, f32[144,432]{1,0:T(8,128)S(1)}, f32[144,432]{1,0:T(8,128)S(1)}...) custom-call(s32[1,16]{1,0:T(1,128)S(1)} %bitcast.46, s32[1,1]{1,0:T(1,128)S(6)} %copy.66.count_ref, ...), custom_call_target="tpu_custom_call" | custom-call | tf_op jit(solution)/shard_map/section/pallas_call | solution.py:595
  108.7 1.3 %reshape.106 = f32[3,48,9,48]{1,0,3,2:T(4,128)} reshape(f32[144,432]{0,1:T(8,128)S(1)} %copy.54) | data formatting | bytes 497664 | tf_op jit(solution)/shard_map/reshape | solution.py:673
  110.0 2.8 %rev.22 = f32[3,48,9,48]{1,0,3,2:T(4,128)S(1)} reverse(f32[3,48,9,48]{1,0,3,2:T(4,128)} %reshape.106), dimensions={0} | reverse | bytes 497664 | tf_op jit(solution)/shard_map/rev | solution.py:673
  112.8 1.1 copy.55
  114.5 1.6 %rev.23 = f32[3,48,9,48]{1,0,3,2:T(4,128)S(1)} reverse(f32[3,48,9,48]{1,0,3,2:T(4,128)S(1)} %reshape.110), dimensions={0} | reverse | bytes 497664 | tf_op jit(solution)/shard_map/rev | solution.py:673
  116.1 1.1 copy.58
  117.4 0.8 copy.56
  118.4 0.7 copy.59
  119.1 0.9 copy.67
  120.0 0.9 copy.68
  (43 shorter events, 5.7 us)
Async XLA Ops:
  3.5 1.0 copy-start.10
  5.0 1.0 copy-start.11
  8.6 0.9 copy-start.13
  8.6 1.7 %copy-start.12 = (bf16[8,48,48]{2,1,0:T(8,128)(2,1)S(1)}, bf16[8,48,48]{2,1,0:T(8,128)(2,1)}, u32[]{:S(2)}) copy-start(bf16[8,48,48]{2,1,0:T(8,128)(2,1)} %param.15) | copy-start | bytes 110596
  8.7 4.7 %copy-start = (bf16[1,1,16,48,512]{4,3,2,1,0:T(8,128)(2,1)S(1)}, bf16[1,1,16,48,512]{4,3,2,1,0:T(8,128)(2,1)}, u32[]{:S(2)}) copy-start(bf16[1,1,16,48,512]{4,3,2,1,0:T(8,128)(2,1)} %param.8) | copy-start | bytes 2359300
  13.4 0.7 copy-start.9
  14.1 0.8 copy-start.1
  14.9 0.8 copy-start.2
  15.7 0.8 copy-start.3
  16.5 0.8 copy-start.4
  107.2 0.6 copy-start.5
  107.9 0.6 copy-start.7
  116.1 1.1 copy-start.8
  117.4 0.9 copy-start.6

commit v2 on v1

--- a/solution.py
+++ b/solution.py
@@ -91,26 +91,23 @@
 
 
 def to_grid(blocks, work, e_ref, grid):
-    @pl.loop(0, 8)
-    def _(t):
-        lanes = pl.ds(pl.multiple_of(t * LANE, LANE), LANE)
+    for t in range(8):
+        lanes = slice(t * LANE, (t + 1) * LANE)
         for pair in range(4):
             one = blocks[2 * t, :, pair * LANE : (pair + 1) * LANE]
             two = blocks[2 * t + 1, :, pair * LANE : (pair + 1) * LANE]
             work[2 * pair, :, lanes] = jnp.concatenate([one[:, :64], two[:, :64]], axis=1)
             work[2 * pair + 1, :, lanes] = jnp.concatenate([one[:, 64:], two[:, 64:]], axis=1)
 
-    @pl.loop(0, 4)
-    def _(n):
-        lanes = pl.ds(pl.multiple_of(n * 256, 256), 256)
+    for n in range(4):
+        lanes = slice(n * 256, (n + 1) * 256)
         moved = dot(work[...].reshape(8 * C, 1024), e_ref[:, lanes])
         grid[:, :, lanes] = moved.astype(BF16).reshape(8, C, 256)
 
 
 def to_blocks(grid, e_ref, blocks):
-    @pl.loop(0, 4)
-    def _(n):
-        rows = pl.ds(pl.multiple_of(n * 256, 256), 256)
+    for n in range(4):
+        rows = slice(n * 256, (n + 1) * 256)
         moved = dot_t(grid[...].reshape(8 * C, 1024), e_ref[rows, :])
         moved = moved.astype(BF16).reshape(8, C, 256)
         for pair in range(4):
@@ -159,42 +156,30 @@
     put(rows, halo, 0, pl.ds((count + 1) * LANE, LANE))
     halo = unpack_edges(received, 1, left_ok, right_ok, depth)
 
-    @pl.loop(0, count)
-    def _(x):
-        rows = grid[:, :, pl.ds(pl.multiple_of(x * LANE, LANE), LANE)].reshape(depth * C, LANE)
-        put(rows, halo, x, pl.ds(pl.multiple_of((x + 1) * LANE, LANE), LANE))
-
-
-def window(wide, z, first):
+    for x in range(count):
+        rows = grid[:, :, x * LANE : (x + 1) * LANE].reshape(depth * C, LANE)
+        put(rows, halo, x, pl.ds((x + 1) * LANE, LANE))
+
+
+def window(wide, z, first, width):
     return jnp.concatenate(
-        [wide[z, :, pl.ds(pl.multiple_of(first + dx * LANE, LANE), 256)] for dx in range(3)], axis=0
+        [wide[z, :, first + dx * LANE : first + dx * LANE + width] for dx in range(3)], axis=0
     )
 
 
 def convolve(wide, weight, total, depth, width):
     total[...] = jnp.zeros_like(total)
-
-    @pl.loop(0, depth)
-    def _(z):
-        @pl.loop(0, width // 256)
-        def _(n):
-            first = pl.multiple_of(n * 256, 256)
-            piece = dot(weight[...], window(wide, z, first)).reshape(3, C, 256)
-            lanes = pl.ds(first, 256)
-            total[pl.ds(z, 3), :, lanes] = total[pl.ds(z, 3), :, lanes] + piece
+    for z in range(depth):
+        for first in range(0, width, 256):
+            piece = dot(weight[...], window(wide, z, first, 256)).reshape(3, C, 256)
+            lanes = slice(first, first + 256)
+            total[z : z + 3, :, lanes] = total[z : z + 3, :, lanes] + piece
 
 
 def kernel_terms(grad, wide, total, depth, width):
-    total[...] = jnp.zeros_like(total)
-
-    @pl.loop(0, depth)
-    def _(z):
-        @pl.loop(0, width // 256)
-        def _(n):
-            first = pl.multiple_of(n * 256, 256)
-            lanes = pl.ds(first, 256)
-            ahead = grad[pl.ds(z, 3), :, lanes].reshape(3 * C, 256)
-            total[...] = total[...] + dot_t(ahead, window(wide, z, first))
+    ahead = [grad[z : z + 3].reshape(3 * C, width) for z in range(depth)]
+    pieces = [window(wide, z, 0, width) for z in range(depth)]
+    total[...] = dot_t(jnp.concatenate(ahead, axis=1), jnp.concatenate(pieces, axis=1))
 
 
 def quarters(grid, wz):

time: 123 us -> 107 us (0.87)
  Pallas kernels: 89.9 us -> 74.2 us
    pallas_call x1, Pallas kernels: 89.9 us -> 74.2 us  [on_device(): pl.pallas_call(section, out_shape=(jax.ShapeDtypeStruct(blocks, BF16), ja...]
where the time goes in v2:
time: 107 us; the launch traced here: 105 us
  Pallas kernels  74.2 us (69%)
  local copies, waits for them, and re-layouts  29.4 us (27%)
  between operations  1.57 us (1%)
    pallas_call x1, Pallas kernels, on_device(): pl.pallas_call(section, out_shape=(jax.ShapeDtypeStruct(blocks, BF16), ja...  74.2 us
    unnamed x30, local copies, waits for them, and re-layouts  9.4 us
    rev x2, local copies, waits for them, and re-layouts, kernel_grad(): rows.reshape(3, C, 9, C)[::-1].transpose(1, 0, 2, 3).reshape(C, 27, C)  4.4 us
    rev x2, local copies, waits for them, and re-layouts, forward_rows(): weight.reshape(C, 3, 9, C)[:, ::-1].transpose(1, 0, 2, 3)  2.71 us
    reshape x8, local copies, waits for them, and re-layouts, forward_rows(): weight.reshape(C, 3, 9, C)[:, ::-1].transpose(1, 0, 2, 3)  2.5 us
    transpose x2, local copies, waits for them, and re-layouts, kernel_grad(): rows.reshape(3, C, 9, C)[::-1].transpose(1, 0, 2, 3).reshape(C, 27, C)  2.22 us

profile of v2, /device:TPU:1, one launch (start us, length us, event | category | flops | bytes accessed | tf_op | source)
XLA Modules:
  0.0 105.1 jit_solution(9594709126901231256)
XLA Ops:
  0.6 1.2 %copy.42 = bf16[48,3,9,48]{0,1,3,2:T(4,128)(2,1)S(1)} copy(bf16[48,3,9,48]{3,0,2,1:T(8,128)(2,1)} %bitcast.51) | data formatting | bytes 248832 | tf_op jit(solution)/shard_map/reshape | solution.py:563
  1.9 1.4 %rev.18 = bf16[48,3,9,48]{0,1,3,2:T(4,128)(2,1)S(1)} reverse(bf16[48,3,9,48]{0,1,3,2:T(4,128)(2,1)S(1)} %copy.42), dimensions={1} | reverse | bytes 248832 | tf_op jit(solution)/shard_map/rev | solution.py:563
  3.6 0.9 copy-done.10
  5.1 0.9 copy-done.11
  6.3 1.4 %rev.20 = bf16[48,3,9,48]{0,1,3,2:T(4,128)(2,1)S(1)} reverse(bf16[48,3,9,48]{0,1,3,2:T(4,128)(2,1)S(1)} %copy.44), dimensions={1} | reverse | bytes 248832 | tf_op jit(solution)/shard_map/rev | solution.py:563
  8.7 0.7 copy-done.13
  9.6 0.7 reshape.100.dga
  10.4 0.7 reshape.102.uup
  11.3 0.7 reshape.103.ugr
  12.0 0.7 reshape.99.ddn
  14.1 0.8 copy-done.1
  14.9 0.8 copy-done.2
  15.7 0.8 copy-done.3
  16.5 0.8 copy-done.4
  17.3 74.2 %section.1 = (bf16[16,48,512]{2,1,0:T(8,128)(2,1)S(1)}, bf16[16,48,512]{2,1,0:T(8,128)(2,1)S(1)}, f32[144,432]{1,0:T(8,128)S(1)}, f32[144,432]{1,0:T(8,128)S(1)}...) custom-call(s32[1,16]{1,0:T(1,128)S(1)} %bitcast.46, s32[1,1]{1,0:T(1,128)S(6)} %copy.66.count_ref, ...), custom_call_target="tpu_custom_call" | custom-call | tf_op jit(solution)/shard_map/section/pallas_call | solution.py:580
  92.9 1.3 %reshape.106 = f32[3,48,9,48]{1,0,3,2:T(4,128)} reshape(f32[144,432]{0,1:T(8,128)S(1)} %copy.54) | data formatting | bytes 497664 | tf_op jit(solution)/shard_map/reshape | solution.py:658
  94.2 2.8 %rev.22 = f32[3,48,9,48]{1,0,3,2:T(4,128)S(1)} reverse(f32[3,48,9,48]{1,0,3,2:T(4,128)} %reshape.106), dimensions={0} | reverse | bytes 497664 | tf_op jit(solution)/shard_map/rev | solution.py:658
  97.0 1.1 %copy.55 = f32[48,3,9,48]{3,0,2,1:T(8,128)} copy(f32[48,3,9,48]{0,1,3,2:T(4,128)S(1)} %bitcast.47) | data formatting | bytes 497664 | tf_op jit(solution)/shard_map/transpose | solution.py:658
  98.7 1.6 %rev.23 = f32[3,48,9,48]{1,0,3,2:T(4,128)S(1)} reverse(f32[3,48,9,48]{1,0,3,2:T(4,128)S(1)} %reshape.110), dimensions={0} | reverse | bytes 497664 | tf_op jit(solution)/shard_map/rev | solution.py:658
  100.3 1.1 %copy.58 = f32[48,3,9,48]{3,0,2,1:T(8,128)} copy(f32[48,3,9,48]{0,1,3,2:T(4,128)S(1)} %bitcast.48) | data formatting | bytes 497664 | tf_op jit(solution)/shard_map/transpose | solution.py:658
  101.6 0.8 copy.56
  102.6 0.7 copy.59
  103.3 0.9 copy.67
  104.2 0.9 copy.68
  (43 shorter events, 5.7 us)
Async XLA Ops:
  3.5 1.0 copy-start.10
  5.0 1.0 copy-start.11
  8.6 0.9 copy-start.13
  8.6 1.7 %copy-start.12 = (bf16[8,48,48]{2,1,0:T(8,128)(2,1)S(1)}, bf16[8,48,48]{2,1,0:T(8,128)(2,1)}, u32[]{:S(2)}) copy-start(bf16[8,48,48]{2,1,0:T(8,128)(2,1)} %param.15) | copy-start | bytes 110596
  8.7 4.7 %copy-start = (bf16[1,1,16,48,512]{4,3,2,1,0:T(8,128)(2,1)S(1)}, bf16[1,1,16,48,512]{4,3,2,1,0:T(8,128)(2,1)}, u32[]{:S(2)}) copy-start(bf16[1,1,16,48,512]{4,3,2,1,0:T(8,128)(2,1)} %param.8) | copy-start | bytes 2359300
  13.4 0.7 copy-start.9
  14.1 0.8 copy-start.1
  14.9 0.8 copy-start.2
  15.7 0.8 copy-start.3
  16.5 0.8 copy-start.4
  91.4 0.6 copy-start.5
  92.1 0.6 copy-start.7
  100.3 1.1 %copy-start.8 = (f32[96,192]{1,0:T(8,128)S(1)}, f32[96,192]{1,0:T(8,128)}, u32[]{:S(2)}) copy-start(f32[96,192]{1,0:T(8,128)} %copy-done.7) | copy-start | bytes 221188
  101.6 0.9 copy-start.6

commit v3 on v2

--- a/solution.py
+++ b/solution.py
@@ -12,8 +12,8 @@
 LANE = 128
 NX = 16
 NY = 16
-ROWS = 1536
-CHUNK = ROWS // NX
+ROWS = 768
+CHUNK = ROWS // NY
 F32 = jnp.float32
 BF16 = jnp.bfloat16
 MESH = pl.DeviceIdType.MESH
@@ -209,6 +209,28 @@
     return jnp.concatenate(parts, axis=1)
 
 
+def kernel_rows(weight, stack, eye, forward, backward):
+    for dz in range(3):
+        for k in range(9):
+            block = weight[9 * dz + k]
+            forward[(2 - dz) * C : (3 - dz) * C, k * C : (k + 1) * C] = block
+            stack[(8 - k) * C : (9 - k) * C, :] = block
+        backward[dz * C : (dz + 1) * C, :] = dot_t(eye[0:C, 0:C], stack[...]).astype(BF16)
+
+
+def step_rows(down, up, stage, eye, ddn, dga, uup, ugr):
+    for o in range(C):
+        stage[8 * o : 8 * o + 8, 0:C] = down[o].astype(F32)
+    for k in range(4):
+        for e in range(2):
+            q = 2 * k + e
+            block = stage[pl.ds(q, C, stride=8), :].astype(BF16)[:, 0:C]
+            ddn[e * C : (e + 1) * C, k * C : (k + 1) * C] = block
+            uup[k * C : (k + 1) * C, e * C : (e + 1) * C] = up[q]
+    dga[...] = dot_t(eye[...], ddn[...]).astype(BF16)
+    ugr[...] = dot_t(eye[0 : 2 * C, 0 : 2 * C], uup[...]).astype(BF16)
+
+
 def slope(value):
     sigma = jax.nn.sigmoid(value)
     return sigma * (1.0 + value * (1.0 - sigma))
@@ -217,8 +239,23 @@
 def section(
     slots_ref,
     count_ref,
-    feat_hbm,
+    feat,
     cot_hbm,
+    fine_hbm,
+    down_hbm,
+    coarse_hbm,
+    up_hbm,
+    blocks_out,
+    blocks_ig,
+    sums,
+    cot_in,
+    fine_w,
+    down_w,
+    coarse_w,
+    up_w,
+    stage,
+    stack,
+    eye,
     wf,
     wfb,
     wc,
@@ -227,14 +264,6 @@
     dga,
     uup,
     ugr,
-    out_hbm,
-    ig_hbm,
-    gf_out,
-    gc_out,
-    gu_out,
-    gd_out,
-    feat,
-    cot_in,
     work,
     places,
     shift_f,
@@ -257,12 +286,8 @@
     ghid,
     ghid3,
     result,
-    blocks_out,
-    blocks_ig,
     term_f,
     term_c,
-    term_u,
-    term_d,
     packed,
     sides_f,
     sides_c,
@@ -271,7 +296,6 @@
     first_in,
     chunk,
     second_in,
-    done,
     local_sem,
     send_sem,
     recv_sem,
@@ -282,10 +306,20 @@
     gy = lax.axis_index("gy")
     here = (gx, gy)
 
-    load_feat = pltpu.make_async_copy(feat_hbm, feat, local_sem.at[0])
-    load_cot = pltpu.make_async_copy(cot_hbm, cot_in, local_sem.at[1])
-    load_feat.start()
-    load_cot.start()
+    loads = [
+        pltpu.make_async_copy(source, target, local_sem.at[k])
+        for k, (source, target) in enumerate(
+            (
+                (fine_hbm, fine_w),
+                (down_hbm, down_w),
+                (coarse_hbm, coarse_w),
+                (up_hbm, up_w),
+                (cot_hbm, cot_in),
+            )
+        )
+    ]
+    for load in loads:
+        load.start()
 
     barrier = pltpu.get_barrier_semaphore()
 
@@ -309,10 +343,7 @@
 
     live_count = count_ref[0, 0]
     build_places(places, slots_ref, live_count)
-    build_shift(shift_f, 8, 127)
-    build_shift(shift_c, 4, 63)
     build_edge(edge_f, 1024, 127)
-    build_edge(edge_c, 512, 63)
     live = live_lanes(slots_ref, live_count)
     half_live = jnp.where(iota((8, LANE), 1) < 64, live, 0.0)
     lower = jnp.where(iota((8, LANE), 1) < 64, 1.0, 0.0)
@@ -351,13 +382,21 @@
             copy.start()
         return copies
 
-    load_feat.wait()
     to_grid(feat, work, places, fine)
     pack_edges(fine[...], 8, edge_f, packed.at[0])
     pl.semaphore_wait(barrier, 2 * (NX - 1) + 4)
     copies = exchange(0, fine, 8, 8, sides_f.at[0])
 
-    load_cot.wait()
+    build_shift(shift_f, 8, 127)
+    build_shift(shift_c, 4, 63)
+    build_edge(edge_c, 512, 63)
+    for load in loads:
+        load.wait()
+    eye[...] = one_hot(iota((4 * C, 4 * C), 0) == iota((4 * C, 4 * C), 1))
+    stage[...] = jnp.zeros_like(stage)
+    kernel_rows(fine_w, stack, eye, wf, wfb)
+    kernel_rows(coarse_w, stack, eye, wc, wcb)
+    step_rows(down_w, up_w, stage, eye, ddn, dga, uup, ugr)
     to_grid(cot_in, work, places, cot)
     for wz in range(4):
         both = dot(ugr[...], quarters(cot, wz))
@@ -398,6 +437,78 @@
 
     pack_edges(gcoarse[1:5], 4, edge_c, packed.at[2])
     copies = exchange(2, gcoarse.at[pl.ds(1, 4)], 4, 4, sides_c.at[1])
+
+    def chunk_rows(index):
+        return pl.ds(pl.multiple_of(index * CHUNK, CHUNK), CHUNK)
+
+    def reduction(part):
+        def first(d):
+            peer = lax.rem(gy + d, NY)
+            return pltpu.make_async_remote_copy(
+                src_ref=grads.at[part, chunk_rows(peer)],
+                dst_ref=first_in.at[part, d],
+                send_sem=sum_send.at[part, 0, d],
+                recv_sem=sum_recv.at[part, 0, d],
+                device_id=(gx, peer),
+                device_id_type=MESH,
+            )
+
+        def second(d):
+            return pltpu.make_async_remote_copy(
+                src_ref=chunk.at[part, 0],
+                dst_ref=second_in.at[part, d],
+                send_sem=sum_send.at[part, 1, d],
+                recv_sem=sum_recv.at[part, 1, d],
+                device_id=(lax.rem(gx + d, NX), gy),
+                device_id_type=MESH,
+            )
+
+        def third(d):
+            return pltpu.make_async_remote_copy(
+                src_ref=chunk.at[part, 1],
+                dst_ref=sums.at[part, chunk_rows(gy)],
+                send_sem=sum_send.at[part, 2, d],
+                recv_sem=sum_recv.at[part, 2, d],
+                device_id=(gx, lax.rem(gy + d, NY)),
+                device_id_type=MESH,
+            )
+
+        return first, second, third
+
+    def start_all(copy):
+        @pl.loop(1, NX)
+        def _(d):
+            copy(d).start()
+
+    def wait_all(copy):
+        @pl.loop(1, NX)
+        def _(d):
+            copy(d).wait()
+
+    def start_second(part):
+        own = grads[part, chunk_rows(gy), :].astype(F32)
+        for d in range(1, NY):
+            own = own + first_in[part, d].astype(F32)
+        chunk[part, 0] = own.astype(BF16)
+        start_all(reductions[part][1])
+        return own
+
+    def start_third(part, own):
+        for d in range(1, NX):
+            own = own + second_in[part, d].astype(F32)
+        chunk[part, 1] = own.astype(BF16)
+        start_all(reductions[part][2])
+        sums[part, chunk_rows(gy), :] = chunk[part, 1]
+
+    def put_rows(part, term):
+        for k in range(4):
+            wide = min(LANE, 9 * C - k * LANE)
+            grads[part, 3 * C * k : 3 * C * (k + 1), 0:wide] = term[
+                :, k * LANE : k * LANE + wide
+            ].astype(BF16)
+
+    reductions = [reduction(0), reduction(1)]
+    grads[...] = jnp.zeros_like(grads)
 
     for wz in range(4):
         upward = dot(uup[...], rect2[wz])
@@ -410,14 +521,14 @@
                     result[2 * wz + a, :, lanes] = (
                         hidden[2 * wz + a + 1, :, lanes] + piece
                     ).astype(BF16)
-    to_blocks(result, places, blocks_out)
-    store_out = pltpu.make_async_copy(blocks_out, out_hbm, local_sem.at[2])
-    store_out.start()
     kernel_terms(gcoarse, low3, term_c, 4, 512)
     total = jnp.zeros((4 * C, 2 * C), F32)
     for wz in range(4):
         total = total + dot_t(quarters(cot, wz), rect2[wz])
-    term_u[...] = total
+    put_rows(0, term_c)
+    grads[0, 12 * C : 16 * C, 0 : 2 * C] = total.astype(BF16)
+    start_all(reductions[0][0])
+    to_blocks(result, places, blocks_out)
 
     for copy in copies:
         copy.wait()
@@ -446,152 +557,102 @@
     pack_edges(ghid[1:9], 8, edge_f, packed.at[3])
     copies = exchange(3, ghid.at[pl.ds(1, 8)], 8, 8, sides_f.at[1])
 
+    wait_all(reductions[0][0])
+    early = start_second(0)
     total = jnp.zeros((2 * C, 4 * C), F32)
     for wz in range(4):
         total = total + dot_t(gdown2[wz], quarters(act, wz))
-    term_d[...] = total
+    grads[1, 12 * C : 14 * C, :] = total[:, 0:LANE].astype(BF16)
+    grads[1, 14 * C : 16 * C, 0:64] = total[:, LANE:192].astype(BF16)
     kernel_terms(ghid, fine3, term_f, 8, 1024)
-
-    grads[...] = jnp.zeros_like(grads)
-    for k in range(4):
-        wide = min(LANE, 432 - k * LANE)
-        lanes = slice(k * LANE, k * LANE + wide)
-        grads[144 * k : 144 * k + 144, 0:wide] = term_f[:, lanes].astype(BF16)
-        grads[576 + 144 * k : 720 + 144 * k, 0:wide] = term_c[:, lanes].astype(BF16)
-    grads[1152:1344, 0:96] = term_u[...].astype(BF16)
-    grads[1344:1440, :] = term_d[:, 0:LANE].astype(BF16)
-    grads[1440:1536, 0:64] = term_d[:, LANE:192].astype(BF16)
-
-    def chunk_rows(index):
-        return pl.ds(pl.multiple_of(index * CHUNK, CHUNK), CHUNK)
-
-    def first_copy(d):
-        peer = lax.rem(gx + d, NX)
-        return pltpu.make_async_remote_copy(
-            src_ref=grads.at[chunk_rows(peer)],
-            dst_ref=first_in.at[d],
-            send_sem=sum_send.at[0, d],
-            recv_sem=sum_recv.at[0, d],
-            device_id=(peer, gy),
-            device_id_type=MESH,
-        )
-
-    def second_copy(d):
-        return pltpu.make_async_remote_copy(
-            src_ref=chunk.at[0],
-            dst_ref=second_in.at[d],
-            send_sem=sum_send.at[1, d],
-            recv_sem=sum_recv.at[1, d],
-            device_id=(gx, lax.rem(gy + d, NY)),
-            device_id_type=MESH,
-        )
-
-    def third_copy(d):
-        return pltpu.make_async_remote_copy(
-            src_ref=chunk.at[1],
-            dst_ref=done.at[chunk_rows(gx)],
-            send_sem=sum_send.at[2, d],
-            recv_sem=sum_recv.at[2, d],
-            device_id=(lax.rem(gx + d, NX), gy),
-            device_id_type=MESH,
-        )
-
-    @pl.loop(1, NX)
-    def _(d):
-        first_copy(d).start()
+    put_rows(1, term_f)
+    start_all(reductions[1][0])
 
     for copy in copies:
         copy.wait()
     widen(ghid.at[pl.ds(1, 8)], sides_f.at[1], edges_in.at[3], shift_f, ghid3, 8, 8, here)
     convolve(ghid3, wfb, hidden, 8, 1024)
 
-    @pl.loop(1, NX)
-    def _(d):
-        first_copy(d).wait()
-
-    own = grads[chunk_rows(gx), :].astype(F32)
-    own = lax.fori_loop(1, NX, lambda d, acc: acc + first_in[d].astype(F32), own)
-    chunk[0] = own.astype(BF16)
-
-    @pl.loop(1, NY)
-    def _(d):
-        second_copy(d).start()
-
-    @pl.loop(0, 8)
-    def _(z):
+    wait_all(reductions[1][0])
+    late = start_second(1)
+    wait_all(reductions[0][1])
+    start_third(0, early)
+
+    for z in range(8):
         result[z] = hidden[z + 1].astype(BF16)
-
     to_blocks(result, places, blocks_ig)
-    store_ig = pltpu.make_async_copy(blocks_ig, ig_hbm, local_sem.at[3])
-    store_ig.start()
-
-    @pl.loop(1, NY)
-    def _(d):
-        second_copy(d).wait()
-
-    own = lax.fori_loop(1, NY, lambda d, acc: acc + second_in[d].astype(F32), own)
-    chunk[1] = own.astype(BF16)
-
-    @pl.loop(1, NX)
-    def _(d):
-        third_copy(d).start()
-
-    done[chunk_rows(gx), :] = chunk[1]
-
-    @pl.loop(1, NX)
-    def _(d):
-        third_copy(d).wait()
-
+
+    wait_all(reductions[1][1])
+    start_third(1, late)
+    wait_all(reductions[0][2])
+    wait_all(reductions[1][2])
+
+
+def unpack(sums, out_in, ig_in, out_hbm, ig_hbm, gf, gd, gc, gu, stage, sem):
+    copies = [
+        pltpu.make_async_copy(out_in, out_hbm, sem.at[0]),
+        pltpu.make_async_copy(ig_in, ig_hbm, sem.at[1]),
+    ]
+    for copy in copies:
+        copy.start()
     scale = 1.0 / math.sqrt(SLOTS * 512 * NX * NY)
+
+    for part, target in ((1, gf), (0, gc)):
+        rows = jnp.concatenate(
+            [sums[part, 3 * C * k : 3 * C * (k + 1), :] for k in range(4)], axis=1
+        )
+        rows = rows.astype(F32) * scale
+        for dz in range(3):
+            for k in range(9):
+                block = rows[(2 - dz) * C : (3 - dz) * C, k * C : (k + 1) * C]
+                target[9 * dz + k] = block
+    tail = sums[1, 14 * C : 16 * C, :]
+    rows = jnp.concatenate([sums[1, 12 * C : 14 * C, :], tail, tail], axis=1)
+    rows = rows.astype(F32) * scale
     for k in range(4):
-        wide = min(LANE, 432 - k * LANE)
-        lanes = slice(k * LANE, k * LANE + wide)
-        gf_out[:, lanes] = done[144 * k : 144 * k + 144, 0:wide].astype(F32) * scale
-        gc_out[:, lanes] = done[576 + 144 * k : 720 + 144 * k, 0:wide].astype(F32) * scale
-    gu_out[...] = done[1152:1344, 0:96].astype(F32) * scale
-    gd_out[:, 0:LANE] = done[1344:1440, :].astype(F32) * scale
-    gd_out[:, LANE:192] = done[1440:1536, 0:64].astype(F32) * scale
-    store_out.wait()
-    store_ig.wait()
+        for e in range(2):
+            gu[2 * k + e] = (
+                sums[0, (12 + k) * C : (13 + k) * C, e * C : (e + 1) * C].astype(F32) * scale
+            )
+            block = rows[e * C : (e + 1) * C, k * C : k * C + LANE]
+            stage[pl.ds(2 * k + e, C, stride=8), :] = block
+    for o in range(C):
+        gd[o] = stage[8 * o : 8 * o + 8, 0:C]
+    for copy in copies:
+        copy.wait()
 
 
 def on_device(
     features, block_slots, block_count, cotangent, fine_weight, down_weight, coarse_weight, up_weight
 ):
-    def forward_rows(weight):
-        return (
-            weight.reshape(C, 3, 9, C)[:, ::-1].transpose(1, 0, 2, 3).reshape(3 * C, 9 * C)
-        )
-
-    def backward_rows(weight):
-        return weight.reshape(C, 3, 9, C)[:, :, ::-1].transpose(1, 3, 2, 0).reshape(3 * C, 9 * C)
-
-    down = down_weight.reshape(C, 4, 2, C)
-    ddn = down.transpose(2, 0, 1, 3).reshape(2 * C, 4 * C)
-    dga = down.transpose(1, 3, 2, 0).reshape(4 * C, 2 * C)
-    up = up_weight.reshape(4, 2, C, C)
-    uup = up.transpose(0, 2, 1, 3).reshape(4 * C, 2 * C)
-    ugr = up.transpose(1, 3, 0, 2).reshape(2 * C, 4 * C)
-
     vmem = pl.BlockSpec(memory_space=pltpu.VMEM)
     smem = pl.BlockSpec(memory_space=pltpu.SMEM)
-    anywhere = pl.BlockSpec(memory_space=pl.ANY)
+    hbm = pl.BlockSpec(memory_space=pltpu.HBM)
     blocks = (SLOTS, C, 512)
-    out, ig, gf, gc, gu, gd = pl.pallas_call(
+    kernel_shape = (27, C, C)
+    block_shape = jax.ShapeDtypeStruct(blocks, BF16)
+    out, ig, sums = pl.pallas_call(
         section,
-        out_shape=(
-            jax.ShapeDtypeStruct(blocks, BF16),
-            jax.ShapeDtypeStruct(blocks, BF16),
-            jax.ShapeDtypeStruct((3 * C, 9 * C), F32),
-            jax.ShapeDtypeStruct((3 * C, 9 * C), F32),
-            jax.ShapeDtypeStruct((4 * C, 2 * C), F32),
-            jax.ShapeDtypeStruct((2 * C, 4 * C), F32),
-        ),
-        in_specs=[smem, smem, anywhere, anywhere] + [vmem] * 8,
-        out_specs=(anywhere, anywhere, vmem, vmem, vmem, vmem),
+        out_shape=(block_shape, block_shape, jax.ShapeDtypeStruct((2, ROWS, LANE), BF16)),
+        in_specs=[smem, smem, vmem] + [hbm] * 5,
+        out_specs=(vmem, vmem, vmem),
         scratch_shapes=[
             pltpu.VMEM(blocks, BF16),
-            pltpu.VMEM(blocks, BF16),
+            pltpu.VMEM(kernel_shape, BF16),
+            pltpu.VMEM((C, 8, C), BF16),
+            pltpu.VMEM(kernel_shape, BF16),
+            pltpu.VMEM((8, C, C), BF16),
+            pltpu.VMEM((8 * C, LANE), F32),
+            pltpu.VMEM((9 * C, C), BF16),
+            pltpu.VMEM((4 * C, 4 * C), BF16),
+            pltpu.VMEM((3 * C, 9 * C), BF16),
+            pltpu.VMEM((3 * C, 9 * C), BF16),
+            pltpu.VMEM((3 * C, 9 * C), BF16),
+            pltpu.VMEM((3 * C, 9 * C), BF16),
+            pltpu.VMEM((2 * C, 4 * C), BF16),
+            pltpu.VMEM((4 * C, 2 * C), BF16),
+            pltpu.VMEM((4 * C, 2 * C), BF16),
+            pltpu.VMEM((2 * C, 4 * C), BF16),
             pltpu.VMEM((8, C, 1024), BF16),
             pltpu.VMEM((1024, 1024), BF16),
             pltpu.VMEM((8, 256, 256), BF16),
@@ -614,26 +675,21 @@
             pltpu.VMEM((10, C, 1024), BF16),
             pltpu.VMEM((8, 3 * C, 1280), BF16),
             pltpu.VMEM((8, C, 1024), BF16),
-            pltpu.VMEM(blocks, BF16),
-            pltpu.VMEM(blocks, BF16),
             pltpu.VMEM((3 * C, 9 * C), F32),
             pltpu.VMEM((3 * C, 9 * C), F32),
-            pltpu.VMEM((4 * C, 2 * C), F32),
-            pltpu.VMEM((2 * C, 4 * C), F32),
             pltpu.VMEM((4, C, LANE), BF16),
             pltpu.VMEM((2, 2, 8, C, LANE), BF16),
             pltpu.VMEM((2, 2, 4, C, LANE), BF16),
             pltpu.VMEM((4, 6, C, LANE), BF16),
-            pltpu.VMEM((ROWS, LANE), BF16),
-            pltpu.VMEM((NX, CHUNK, LANE), BF16),
-            pltpu.VMEM((2, CHUNK, LANE), BF16),
-            pltpu.VMEM((NY, CHUNK, LANE), BF16),
-            pltpu.VMEM((ROWS, LANE), BF16),
-            pltpu.SemaphoreType.DMA((4,)),
+            pltpu.VMEM((2, ROWS, LANE), BF16),
+            pltpu.VMEM((2, NY, CHUNK, LANE), BF16),
+            pltpu.VMEM((2, 2, CHUNK, LANE), BF16),
+            pltpu.VMEM((2, NX, CHUNK, LANE), BF16),
+            pltpu.SemaphoreType.DMA((5,)),
             pltpu.SemaphoreType.DMA((4, 8)),
             pltpu.SemaphoreType.DMA((4, 8)),
-            pltpu.SemaphoreType.DMA((3, NX)),
-            pltpu.SemaphoreType.DMA((3, NX)),
+            pltpu.SemaphoreType.DMA((2, 3, NX)),
+            pltpu.SemaphoreType.DMA((2, 3, NX)),
         ],
         compiler_params=pltpu.CompilerParams(
             collective_id=0, has_side_effects=True, vmem_limit_bytes=50 * 1024 * 1024
@@ -644,28 +700,30 @@
         block_count.reshape(1, 1),
         features.reshape(blocks),
         cotangent.reshape(blocks),
-        forward_rows(fine_weight),
-        backward_rows(fine_weight),
-        forward_rows(coarse_weight),
-        backward_rows(coarse_weight),
-        ddn,
-        dga,
-        uup,
-        ugr,
+        fine_weight.transpose(1, 0, 2),
+        down_weight,
+        coarse_weight.transpose(1, 0, 2),
+        up_weight,
     )
-
-    def kernel_grad(rows):
-        return rows.reshape(3, C, 9, C)[::-1].transpose(1, 0, 2, 3).reshape(C, 27, C)
-
+    out, ig, gf, gd, gc, gu = pl.pallas_call(
+        unpack,
+        out_shape=(
+            block_shape,
+            block_shape,
+            jax.ShapeDtypeStruct(kernel_shape, F32),
+            jax.ShapeDtypeStruct((C, 8, C), F32),
+            jax.ShapeDtypeStruct(kernel_shape, F32),
+            jax.ShapeDtypeStruct((8, C, C), F32),
+        ),
+        in_specs=[vmem, vmem, vmem],
+        out_specs=(hbm, hbm, vmem, vmem, vmem, vmem),
+        scratch_shapes=[pltpu.VMEM((8 * C, LANE), F32), pltpu.SemaphoreType.DMA((2,))],
+        compiler_params=pltpu.CompilerParams(vmem_limit_bytes=8 * 1024 * 1024),
+        name="unpack",
+    )(sums, out, ig)
     shape_out = (1, 1) + blocks
-    return (
-        out.reshape(shape_out),
-        ig.reshape(shape_out),
-        kernel_grad(gf),
-        gd.reshape(2, C, 4, C).transpose(1, 2, 0, 3).reshape(C, 8, C),
-        kernel_grad(gc),
-        gu.reshape(4, C, 2, C).transpose(0, 2, 1, 3).reshape(8, C, C),
-    )
+    gf, gc = gf.transpose(1, 0, 2), gc.transpose(1, 0, 2)
+    return out.reshape(shape_out), ig.reshape(shape_out), gf, gd, gc, gu
 
 
 def solution(mesh):

time: 107 us -> 79.7 us (0.74); the launches traced: 105 us -> 79.4 us
  local copies, waits for them, and re-layouts: 29.4 us -> 5.51 us
  Pallas kernels: 74.2 us -> 72.4 us
    reshape x24 -> x0, local copies, waits for them, and re-layouts: 8.45 us -> none  [the longest x8 2.5 us: forward_rows(): weight.reshape(C, 3, 9, C)[:, ::-1].transpose(1, 0, 2, 3)]
    rev x4 -> x0, local copies, waits for them, and re-layouts: 7.11 us -> none  [the longest x2 4.4 us: kernel_grad(): rows.reshape(3, C, 9, C)[::-1].transpose(1, 0, 2, 3).reshape(C, 27, C)]
    transpose x6 -> x0, local copies, waits for them, and re-layouts: 4.07 us -> none  [the longest x2 2.22 us: kernel_grad(): rows.reshape(3, C, 9, C)[::-1].transpose(1, 0, 2, 3).reshape(C, 27, C)]
    unnamed x30 -> x12, local copies, waits for them, and re-layouts: 9.4 us -> 5.51 us
    pallas_call x1 -> x2, Pallas kernels: 74.2 us -> 72.4 us  [the longest x1 69.7 us: on_device(): pl.pallas_call(section, out_shape=(block_shape, block_shape, jax.ShapeDty...]
where the time goes in v3:
time: 79.7 us; the launch traced here: 79.4 us
  Pallas kernels  72.4 us (91%)
  local copies, waits for them, and re-layouts  5.51 us (7%)
  between operations  1.46 us (2%)
    pallas_call x1, Pallas kernels, on_device(): pl.pallas_call(section, out_shape=(block_shape, block_shape, jax.ShapeDty...  69.7 us
    unnamed x12, local copies, waits for them, and re-layouts  5.51 us
    pallas_call x1, Pallas kernels, on_device(): pl.pallas_call(unpack, out_shape=(block_shape, block_shape, jax.ShapeDtyp...  2.65 us

profile of v3, /device:TPU:1, one launch (start us, length us, event | category | flops | bytes accessed | tf_op | source)
XLA Modules:
  0.0 79.4 jit_solution(13165910630770813672)
XLA Ops:
  1.3 0.0 copy-start.5
  1.3 0.6 copy-done.5
  1.9 0.0 copy-start
  1.9 1.1 %copy-done = bf16[1,1,16,48,512]{4,3,2,1,0:T(8,128)(2,1)S(1)} copy-done((bf16[1,1,16,48,512]{4,3,2,1,0:T(8,128)(2,1)S(1)}, bf16[1,1,16,48,512]{4,3,2,1,0:T(8,128)(2,1)}, u32[]{:S(2)}) %copy-start) | copy-done | bytes 786456
  3.1 0.0 copy-start.1
  3.1 1.0 %copy-done.1 = bf16[48,27,48]{2,0,1:T(8,128)(2,1)S(1)} copy-done((bf16[48,27,48]{2,0,1:T(8,128)(2,1)S(1)}, bf16[48,27,48]{2,0,1:T(8,128)(2,1)}, u32[]{:S(2)}) %copy-start.1) | copy-done | bytes 124440
  4.0 0.0 copy-start.2
  4.0 1.0 %copy-done.2 = bf16[48,27,48]{2,0,1:T(8,128)(2,1)S(1)} copy-done((bf16[48,27,48]{2,0,1:T(8,128)(2,1)S(1)}, bf16[48,27,48]{2,0,1:T(8,128)(2,1)}, u32[]{:S(2)}) %copy-start.2) | copy-done | bytes 124440
  5.0 0.0 copy-start.3
  5.0 0.9 %copy-done.3 = bf16[48,8,48]{2,1,0:T(8,128)(2,1)S(1)} copy-done((bf16[48,8,48]{2,1,0:T(8,128)(2,1)S(1)}, bf16[48,8,48]{2,1,0:T(8,128)(2,1)}, u32[]{:S(2)}) %copy-start.3) | copy-done | bytes 36888
  5.9 0.0 copy-start.4
  5.9 0.9 %copy-done.4 = bf16[8,48,48]{2,1,0:T(8,128)(2,1)S(1)} copy-done((bf16[8,48,48]{2,1,0:T(8,128)(2,1)S(1)}, bf16[8,48,48]{2,1,0:T(8,128)(2,1)}, u32[]{:S(2)}) %copy-start.4) | copy-done | bytes 36888
  6.8 69.7 %section.1 = (bf16[16,48,512]{2,1,0:T(8,128)(2,1)S(1)}, bf16[16,48,512]{2,1,0:T(8,128)(2,1)S(1)}, bf16[2,768,128]{2,1,0:T(8,128)(2,1)S(1)}) custom-call(s32[1,16]{1,0:T(1,128)S(1)} %bitcast.12, s32[1,1]{1,0:T(1,128)S(6)} %copy.14.count_ref, bf16[16,48,512]{2,1,0:T(8,128)(2,1)S(1)} %bitcast.9, bf16[16,48,512]{2,1,0:T(8,128)(2,1)} %bitcast.13, ...), custom_call_target="tpu_custom_call" | custom-call | tf_op jit(solution)/shard_map/section/pallas_call | solution.py:634
  76.6 2.7 %unpack.1 = (bf16[16,48,512]{2,1,0:T(8,128)(2,1)}, bf16[16,48,512]{2,1,0:T(8,128)(2,1)}, f32[27,48,48]{2,1,0:T(8,128)}, f32[48,8,48]{2,1,0:T(8,128)}, f32[27,48,48]{2,1,0:T(8,128)}, /*index=5*/f32[8,48,48]{2,1,0:T(8,128)}) custom-call(bf16[2,768,128]{2,1,0:T(8,128)(2,1)S(1)} %get-tuple-element.15.sums, bf16[16,48,512]{2,1,0:T(8,128)(2,1)S(1)} %get-tuple-element.16.out_in, ...), custom_call_target="tpu_custom_call" | custom-call | tf_op jit(solution)/shard_map/unpack/pallas_call | solution.py:708
Async XLA Ops:
  1.3 0.7 copy-start.5
  1.9 1.1 %copy-start = (bf16[1,1,16,48,512]{4,3,2,1,0:T(8,128)(2,1)S(1)}, bf16[1,1,16,48,512]{4,3,2,1,0:T(8,128)(2,1)}, u32[]{:S(2)}) copy-start(bf16[1,1,16,48,512]{4,3,2,1,0:T(8,128)(2,1)} %param.8) | copy-start | bytes 2359300
  3.1 1.0 %copy-start.1 = (bf16[48,27,48]{2,0,1:T(8,128)(2,1)S(1)}, bf16[48,27,48]{2,0,1:T(8,128)(2,1)}, u32[]{:S(2)}) copy-start(bf16[48,27,48]{2,0,1:T(8,128)(2,1)} %param.12) | copy-start | bytes 373252
  4.0 1.0 %copy-start.2 = (bf16[48,27,48]{2,0,1:T(8,128)(2,1)S(1)}, bf16[48,27,48]{2,0,1:T(8,128)(2,1)}, u32[]{:S(2)}) copy-start(bf16[48,27,48]{2,0,1:T(8,128)(2,1)} %param.14) | copy-start | bytes 373252
  5.0 0.9 %copy-start.3 = (bf16[48,8,48]{2,1,0:T(8,128)(2,1)S(1)}, bf16[48,8,48]{2,1,0:T(8,128)(2,1)}, u32[]{:S(2)}) copy-start(bf16[48,8,48]{2,1,0:T(8,128)(2,1)} %down_hbm.1) | copy-start | bytes 110596
  5.9 0.9 %copy-start.4 = (bf16[8,48,48]{2,1,0:T(8,128)(2,1)S(1)}, bf16[8,48,48]{2,1,0:T(8,128)(2,1)}, u32[]{:S(2)}) copy-start(bf16[8,48,48]{2,1,0:T(8,128)(2,1)} %up_hbm.1) | copy-start | bytes 110596

commit v4 on v3

--- a/solution.py
+++ b/solution.py
@@ -12,8 +12,8 @@
 LANE = 128
 NX = 16
 NY = 16
-ROWS = 768
-CHUNK = ROWS // NY
+ROWS_A = 512
+ROWS_B = 1024
 F32 = jnp.float32
 BF16 = jnp.bfloat16
 MESH = pl.DeviceIdType.MESH
@@ -35,33 +35,60 @@
     return jnp.where(cond, 1.0, 0.0).astype(BF16)
 
 
-def build_shift(s_ref, count, last):
+def build_shift_fine(s_ref):
     row = iota((256, 256), 0)
     col = iota((256, 256), 1)
     lane = col % LANE
     right = col >= LANE
-    if last == 127:
-        before = jnp.where(lane < 64, lane + 63, lane - 64)
-        after = jnp.where(lane < 64, lane + 64, lane - 63)
-        before = jnp.where(lane == 0, -1, before)
-        after = jnp.where(lane == 127, -1, after)
-    else:
-        before = jnp.where((lane == 0) | (lane > last), -1, lane - 1)
-        after = jnp.where(lane >= last, -1, lane + 1)
+    before = jnp.where(lane < 64, lane + 63, lane - 64)
+    after = jnp.where(lane < 64, lane + 64, lane - 63)
+    before = jnp.where(lane == 0, -1, before)
+    after = jnp.where(lane == 127, -1, after)
     source = jnp.where(right, after, before)
-    place = jnp.where(lane == jnp.where(right, last, 0), jnp.where(right, LANE + 8, LANE), -512)
-
-    @pl.loop(0, count)
+    place = jnp.where(lane == jnp.where(right, 127, 0), jnp.where(right, LANE + 8, LANE), -512)
+
+    @pl.loop(0, 8)
     def _(x):
         s_ref[x] = one_hot((row == source) | (row == place + x))
 
 
-def build_edge(t_ref, length, last):
-    row = iota((length, LANE), 0)
-    col = iota((length, LANE), 1)
+def coarse_edge(group):
+    return jnp.where(
+        group == 0, 63, jnp.where(group == 1, 62, jnp.where(group == 2, 0, jnp.where(group == 3, 1, -1)))
+    )
+
+
+def build_shift_coarse(s_ref):
+    row = iota((256, 384), 0)
+    col = iota((256, 384), 1)
+    source = (col % LANE + col // LANE + LANE - 1) % LANE
+    halo = row - LANE
+    spot = jnp.where(
+        halo < 4, 127, jnp.where(halo < 8, 126, jnp.where(halo < 12, 64, jnp.where(halo < 16, 65, -1)))
+    )
+    own = (row < 64) & (row == source)
+    other = (halo >= 0) & (spot == source)
+
+    @pl.loop(0, 4)
+    def _(x):
+        s_ref[x] = one_hot(own | (other & (halo % 4 == x)))
+
+
+def build_roll(r_ref):
+    row = iota((LANE, 256), 0)
+    col = iota((LANE, 256), 1)
+    r_ref[...] = one_hot(row == (col % LANE + 2 * (col // LANE) + LANE - 1) % LANE)
+
+
+def build_edges(fine_ref, coarse_ref):
+    row = iota((1024, LANE), 0)
+    col = iota((1024, LANE), 1)
     lane = row % LANE
     x = row // LANE
-    t_ref[...] = one_hot(((lane == last) & (col == x)) | ((lane == 0) & (col == x + 8)))
+    fine_ref[...] = one_hot(((lane == 127) & (col == x)) | ((lane == 0) & (col == x + 8)))
+    row = iota((512, LANE), 0)
+    col = iota((512, LANE), 1)
+    coarse_ref[...] = one_hot((row % LANE == coarse_edge(col // 4)) & (row // LANE == col % 4))
 
 
 def build_places(e_ref, slots_ref, live_count):
@@ -161,6 +188,70 @@
         put(rows, halo, x, pl.ds((x + 1) * LANE, LANE))
 
 
+def coarse_halos(received, place):
+    gx, gy = place
+    left_ok, right_ok = gy > 0, gy < NY - 1
+    low_ok, high_ok = gx > 0, gx < NX - 1
+    return (
+        unpack_edges(received, 0, left_ok & low_ok, right_ok & low_ok, 4),
+        unpack_edges(received, 1, left_ok, right_ok, 4),
+        unpack_edges(received, 2, left_ok & high_ok, right_ok & high_ok, 4),
+    )
+
+
+def widen_coarse(grid, sides, received, s_ref, wide, place):
+    gx = place[0]
+    halos = coarse_halos(received, place)
+    zero = jnp.zeros((4 * C, LANE), BF16)
+    for column in range(8):
+        if column < 2:
+            lanes = slice(column * LANE, (column + 1) * LANE)
+            rows = jnp.where(gx > 0, sides[0, :, :, lanes].reshape(4 * C, LANE), zero)
+            halo, x = halos[0], column + 2
+        elif column < 6:
+            x = column - 2
+            rows = grid[:, :, x * LANE : (x + 1) * LANE].reshape(4 * C, LANE)
+            halo = halos[1]
+        else:
+            x = column - 6
+            lanes = slice(x * LANE, (x + 1) * LANE)
+            rows = jnp.where(gx < NX - 1, sides[1, :, :, lanes].reshape(4 * C, LANE), zero)
+            halo = halos[2]
+        moved = dot(jnp.concatenate([rows, halo], axis=1), s_ref[x]).astype(BF16)
+        for t in range(3):
+            part = moved[:, t * LANE : (t + 1) * LANE].reshape(4, C, LANE)
+            wide[:, t * C : (t + 1) * C, column * LANE : (column + 1) * LANE] = part
+
+
+def extend_grect(grect, sides, received, s_ref, wide, place):
+    gx = place[0]
+    halos = coarse_halos(received, place)
+    zero = jnp.zeros((4 * C, LANE), F32)
+    for column in range(6):
+        if column == 0:
+            rows = jnp.where(gx > 0, sides[0].reshape(4 * C, LANE).astype(F32), zero)
+            halo, x = halos[0], 3
+        elif column < 5:
+            x = column - 1
+            rows = grect[:, :, x * LANE : (x + 1) * LANE].reshape(4 * C, LANE)
+            halo = halos[1]
+        else:
+            rows = jnp.where(gx < NX - 1, sides[1].reshape(4 * C, LANE).astype(F32), zero)
+            halo, x = halos[2], 0
+        total = rows + dot(halo, s_ref[x, LANE:, LANE : 2 * LANE])
+        wide[:, :, column * LANE : (column + 1) * LANE] = total.reshape(4, C, LANE)
+
+
+def roll_columns(grid, r_ref, wide):
+    for column in range(6):
+        lanes = slice(column * LANE, (column + 1) * LANE)
+        rows = grid[:, :, lanes]
+        moved = dot(rows.reshape(4 * C, LANE), r_ref[...]).astype(BF16)
+        wide[:, 0:C, lanes] = moved[:, :LANE].reshape(4, C, LANE)
+        wide[:, C : 2 * C, lanes] = rows
+        wide[:, 2 * C : 3 * C, lanes] = moved[:, LANE:].reshape(4, C, LANE)
+
+
 def window(wide, z, first, width):
     return jnp.concatenate(
         [wide[z, :, first + dx * LANE : first + dx * LANE + width] for dx in range(3)], axis=0
@@ -176,9 +267,9 @@
             total[z : z + 3, :, lanes] = total[z : z + 3, :, lanes] + piece
 
 
-def kernel_terms(grad, wide, total, depth, width):
+def kernel_terms(grad, wide, total, depth, width, start):
     ahead = [grad[z : z + 3].reshape(3 * C, width) for z in range(depth)]
-    pieces = [window(wide, z, 0, width) for z in range(depth)]
+    pieces = [window(wide, z, start, width) for z in range(depth)]
     total[...] = dot_t(jnp.concatenate(ahead, axis=1), jnp.concatenate(pieces, axis=1))
 
 
@@ -239,7 +330,7 @@
 def section(
     slots_ref,
     count_ref,
-    feat,
+    feat_hbm,
     cot_hbm,
     fine_hbm,
     down_hbm,
@@ -247,7 +338,9 @@
     up_hbm,
     blocks_out,
     blocks_ig,
-    sums,
+    sums_a,
+    sums_b,
+    feat,
     cot_in,
     fine_w,
     down_w,
@@ -268,6 +361,7 @@
     places,
     shift_f,
     shift_c,
+    roll_c,
     edge_f,
     edge_c,
     fine,
@@ -278,9 +372,13 @@
     low,
     low3,
     coarse,
+    coarse2,
     grect,
+    grect_low,
+    grect_wide,
     rect2,
     gcoarse,
+    gcoarse_own,
     gcoarse3,
     gdown2,
     ghid,
@@ -291,11 +389,16 @@
     packed,
     sides_f,
     sides_c,
+    sides_g,
     edges_in,
-    grads,
-    first_in,
-    chunk,
-    second_in,
+    grads_a,
+    first_in_a,
+    chunk_a,
+    second_in_a,
+    grads_b,
+    first_in_b,
+    chunk_b,
+    second_in_b,
     local_sem,
     send_sem,
     recv_sem,
@@ -306,6 +409,8 @@
     gy = lax.axis_index("gy")
     here = (gx, gy)
 
+    load_feat = pltpu.make_async_copy(feat_hbm, feat, local_sem.at[5])
+    load_feat.start()
     loads = [
         pltpu.make_async_copy(source, target, local_sem.at[k])
         for k, (source, target) in enumerate(
@@ -343,19 +448,19 @@
 
     live_count = count_ref[0, 0]
     build_places(places, slots_ref, live_count)
-    build_edge(edge_f, 1024, 127)
+    build_edges(edge_f, edge_c)
     live = live_lanes(slots_ref, live_count)
     half_live = jnp.where(iota((8, LANE), 1) < 64, live, 0.0)
     lower = jnp.where(iota((8, LANE), 1) < 64, 1.0, 0.0)
 
-    def exchange(step, source, depth, count, sides):
+    def exchange(step, source, length, width, sides):
         copies = []
         for side in range(2):
-            x = count - 1 if side == 0 else 0
+            first = length - width if side == 0 else 0
             shift = 1 if side == 0 else NX - 1
             copies.append(
                 pltpu.make_async_remote_copy(
-                    src_ref=source.at[:, :, pl.ds(x * LANE, LANE)],
+                    src_ref=source.at[:, :, pl.ds(first, width)],
                     dst_ref=sides.at[side],
                     send_sem=send_sem.at[step, side],
                     recv_sem=recv_sem.at[step, side],
@@ -382,71 +487,17 @@
             copy.start()
         return copies
 
-    to_grid(feat, work, places, fine)
-    pack_edges(fine[...], 8, edge_f, packed.at[0])
-    pl.semaphore_wait(barrier, 2 * (NX - 1) + 4)
-    copies = exchange(0, fine, 8, 8, sides_f.at[0])
-
-    build_shift(shift_f, 8, 127)
-    build_shift(shift_c, 4, 63)
-    build_edge(edge_c, 512, 63)
-    for load in loads:
-        load.wait()
-    eye[...] = one_hot(iota((4 * C, 4 * C), 0) == iota((4 * C, 4 * C), 1))
-    stage[...] = jnp.zeros_like(stage)
-    kernel_rows(fine_w, stack, eye, wf, wfb)
-    kernel_rows(coarse_w, stack, eye, wc, wcb)
-    step_rows(down_w, up_w, stage, eye, ddn, dga, uup, ugr)
-    to_grid(cot_in, work, places, cot)
-    for wz in range(4):
-        both = dot(ugr[...], quarters(cot, wz))
-        grect[wz] = both[:C] + roll_half(both[C:])
-
-    for copy in copies:
-        copy.wait()
-    widen(fine, sides_f.at[0], edges_in.at[0], shift_f, fine3, 8, 8, here)
-    convolve(fine3, wf, hidden, 8, 1024)
-
-    live_fine = tile_lanes(live, C, 1024)
-
-    @pl.loop(0, 8)
-    def _(z):
-        value = hidden[z + 1] * live_fine
-        hidden[z + 1] = value
-        act[z] = (value * jax.nn.sigmoid(value)).astype(BF16)
-
-    lower_mask = tile_lanes(lower, C, 512)
-    for wz in range(4):
-        both = dot(ddn[...], quarters(act, wz))
-        low[wz] = ((both[:C] + roll_half(both[C:])) * lower_mask).astype(BF16)
-
-    pack_edges(low[...], 4, edge_c, packed.at[1])
-    copies = exchange(1, low, 4, 4, sides_c.at[0])
-    for copy in copies:
-        copy.wait()
-    widen(low, sides_c.at[0], edges_in.at[1], shift_c, low3, 4, 4, here)
-    convolve(low3, wc, coarse, 4, 512)
-
-    gcoarse[...] = jnp.zeros_like(gcoarse)
-    for wz in range(4):
-        value = coarse[wz + 1]
-        rect = value * jax.nn.sigmoid(value) * lower_mask
-        rect2[wz, 0:C] = rect.astype(BF16)
-        rect2[wz, C : 2 * C] = roll_half(rect).astype(BF16)
-        gcoarse[wz + 1] = (grect[wz] * slope(value) * lower_mask).astype(BF16)
-
-    pack_edges(gcoarse[1:5], 4, edge_c, packed.at[2])
-    copies = exchange(2, gcoarse.at[pl.ds(1, 4)], 4, 4, sides_c.at[1])
-
-    def chunk_rows(index):
-        return pl.ds(pl.multiple_of(index * CHUNK, CHUNK), CHUNK)
-
-    def reduction(part):
+    def reduction(grads, first_in, chunk, second_in, sums, part):
+        rows = chunk.shape[1]
+
+        def chunk_rows(index):
+            return pl.ds(pl.multiple_of(index * rows, rows), rows)
+
         def first(d):
             peer = lax.rem(gy + d, NY)
             return pltpu.make_async_remote_copy(
-                src_ref=grads.at[part, chunk_rows(peer)],
-                dst_ref=first_in.at[part, d],
+                src_ref=grads.at[chunk_rows(peer)],
+                dst_ref=first_in.at[d],
                 send_sem=sum_send.at[part, 0, d],
                 recv_sem=sum_recv.at[part, 0, d],
                 device_id=(gx, peer),
@@ -455,8 +506,8 @@
 
         def second(d):
             return pltpu.make_async_remote_copy(
-                src_ref=chunk.at[part, 0],
-                dst_ref=second_in.at[part, d],
+                src_ref=chunk.at[0],
+                dst_ref=second_in.at[d],
                 send_sem=sum_send.at[part, 1, d],
                 recv_sem=sum_recv.at[part, 1, d],
                 device_id=(lax.rem(gx + d, NX), gy),
@@ -465,15 +516,38 @@
 
         def third(d):
             return pltpu.make_async_remote_copy(
-                src_ref=chunk.at[part, 1],
-                dst_ref=sums.at[part, chunk_rows(gy)],
+                src_ref=chunk.at[1],
+                dst_ref=sums.at[chunk_rows(gy)],
                 send_sem=sum_send.at[part, 2, d],
                 recv_sem=sum_recv.at[part, 2, d],
                 device_id=(gx, lax.rem(gy + d, NY)),
                 device_id_type=MESH,
             )
 
-        return first, second, third
+        def start_first():
+            start_all(first)
+
+        def start_second():
+            wait_all(first)
+            own = grads[chunk_rows(gy), :].astype(F32)
+            for d in range(1, NY):
+                own = own + first_in[d].astype(F32)
+            chunk[0] = own.astype(BF16)
+            start_all(second)
+            return own
+
+        def start_third(own):
+            wait_all(second)
+            for d in range(1, NX):
+                own = own + second_in[d].astype(F32)
+            chunk[1] = own.astype(BF16)
+            start_all(third)
+            sums[chunk_rows(gy), :] = chunk[1]
+
+        def finish():
+            wait_all(third)
+
+        return start_first, start_second, start_third, finish
 
     def start_all(copy):
         @pl.loop(1, NX)
@@ -485,61 +559,84 @@
         def _(d):
             copy(d).wait()
 
-    def start_second(part):
-        own = grads[part, chunk_rows(gy), :].astype(F32)
-        for d in range(1, NY):
-            own = own + first_in[part, d].astype(F32)
-        chunk[part, 0] = own.astype(BF16)
-        start_all(reductions[part][1])
-        return own
-
-    def start_third(part, own):
-        for d in range(1, NX):
-            own = own + second_in[part, d].astype(F32)
-        chunk[part, 1] = own.astype(BF16)
-        start_all(reductions[part][2])
-        sums[part, chunk_rows(gy), :] = chunk[part, 1]
-
-    def put_rows(part, term):
-        for k in range(4):
-            wide = min(LANE, 9 * C - k * LANE)
-            grads[part, 3 * C * k : 3 * C * (k + 1), 0:wide] = term[
-                :, k * LANE : k * LANE + wide
-            ].astype(BF16)
-
-    reductions = [reduction(0), reduction(1)]
-    grads[...] = jnp.zeros_like(grads)
-
+    def put_rows(grads, term):
+        for k in range(3):
+            grads[3 * C * k : 3 * C * (k + 1), :] = term[:, k * LANE : (k + 1) * LANE].astype(BF16)
+        grads[9 * C : 9 * C + 80, 0:C] = term[0:80, 3 * LANE :].astype(BF16)
+        grads[9 * C : 9 * C + 64, 64 : 64 + C] = term[80:144, 3 * LANE :].astype(BF16)
+
+    load_feat.wait()
+    to_grid(feat, work, places, fine)
+    pack_edges(fine[...], 8, edge_f, packed.at[0])
+    pl.semaphore_wait(barrier, 2 * (NX - 1) + 4)
+    copies = exchange(0, fine, 1024, LANE, sides_f.at[0])
+
+    for load in loads:
+        load.wait()
+    build_shift_coarse(shift_c)
+    to_grid(cot_in, work, places, cot)
+    eye[...] = one_hot(iota((4 * C, 4 * C), 0) == iota((4 * C, 4 * C), 1))
+    stage[...] = jnp.zeros_like(stage)
+    step_rows(down_w, up_w, stage, eye, ddn, dga, uup, ugr)
+    lower_mask = tile_lanes(lower, C, 512)
     for wz in range(4):
-        upward = dot(uup[...], rect2[wz])
-        for a in range(2):
-            for b in range(2):
-                k = 2 * a + b
-                for wx in range(4):
-                    lanes = pl.ds((2 * wx + b) * LANE, LANE)
-                    piece = upward[k * C : (k + 1) * C, wx * LANE : (wx + 1) * LANE]
-                    result[2 * wz + a, :, lanes] = (
-                        hidden[2 * wz + a + 1, :, lanes] + piece
-                    ).astype(BF16)
-    kernel_terms(gcoarse, low3, term_c, 4, 512)
-    total = jnp.zeros((4 * C, 2 * C), F32)
-    for wz in range(4):
-        total = total + dot_t(quarters(cot, wz), rect2[wz])
-    put_rows(0, term_c)
-    grads[0, 12 * C : 16 * C, 0 : 2 * C] = total.astype(BF16)
-    start_all(reductions[0][0])
-    to_blocks(result, places, blocks_out)
+        both = dot(ugr[...], quarters(cot, wz))
+        value = (both[:C] + roll_half(both[C:])) * lower_mask
+        grect[wz] = value
+        grect_low[wz] = value.astype(BF16)
+    pack_edges(grect_low[...], 4, edge_c, packed.at[2])
+    grect_copies = exchange(2, grect_low, 512, LANE, sides_g)
+    build_shift_fine(shift_f)
+    build_roll(roll_c)
+    kernel_rows(fine_w, stack, eye, wf, wfb)
+    kernel_rows(coarse_w, stack, eye, wc, wcb)
+    grads_a[...] = jnp.zeros_like(grads_a)
+    grads_b[...] = jnp.zeros_like(grads_b)
+    gcoarse_own[...] = jnp.zeros_like(gcoarse_own)
 
     for copy in copies:
         copy.wait()
-    widen(gcoarse.at[pl.ds(1, 4)], sides_c.at[1], edges_in.at[2], shift_c, gcoarse3, 4, 4, here)
-    convolve(gcoarse3, wcb, coarse, 4, 512)
+    widen(fine, sides_f.at[0], edges_in.at[0], shift_f, fine3, 8, 8, here)
+    convolve(fine3, wf, hidden, 8, 1024)
+
+    live_fine = tile_lanes(live, C, 1024)
+    for z in range(8):
+        value = hidden[z + 1] * live_fine
+        hidden[z + 1] = value
+        act[z] = (value * jax.nn.sigmoid(value)).astype(BF16)
+
+    for wz in range(4):
+        both = dot(ddn[...], quarters(act, wz))
+        low[wz] = ((both[:C] + roll_half(both[C:])) * lower_mask).astype(BF16)
+
+    pack_edges(low[...], 4, edge_c, packed.at[1])
+    copies = exchange(1, low, 512, 2 * LANE, sides_c)
+    for copy in grect_copies:
+        copy.wait()
+    extend_grect(grect, sides_g, edges_in.at[2], shift_c, grect_wide, here)
+    for copy in copies:
+        copy.wait()
+    widen_coarse(low, sides_c, edges_in.at[1], shift_c, low3, here)
+    convolve(low3, wc, coarse, 4, 768)
+
+    for wz in range(4):
+        value = coarse[wz + 1]
+        grad = grect_wide[wz] * slope(value)
+        gcoarse[wz] = grad.astype(BF16)
+        gcoarse_own[wz + 1] = (grad[:, LANE : 5 * LANE] * lower_mask).astype(BF16)
+        value = value[:, LANE : 5 * LANE]
+        rect = value * jax.nn.sigmoid(value) * lower_mask
+        rect2[wz, 0:C] = rect.astype(BF16)
+        rect2[wz, C : 2 * C] = roll_half(rect).astype(BF16)
+
+    roll_columns(gcoarse, roll_c, gcoarse3)
+    convolve(gcoarse3, wcb, coarse2, 4, 512)
 
     live_coarse = tile_lanes(half_live, C, 512)
     ghid[0] = jnp.zeros((C, 1024), BF16)
     ghid[9] = jnp.zeros((C, 1024), BF16)
     for wz in range(4):
-        value = coarse[wz + 1] * live_coarse
+        value = coarse2[wz + 1] * live_coarse
         gdown2[wz, 0:C] = value.astype(BF16)
         gdown2[wz, C : 2 * C] = roll_half(value).astype(BF16)
         back = dot(dga[...], gdown2[wz])
@@ -555,40 +652,59 @@
                     ).astype(BF16)
 
     pack_edges(ghid[1:9], 8, edge_f, packed.at[3])
-    copies = exchange(3, ghid.at[pl.ds(1, 8)], 8, 8, sides_f.at[1])
-
-    wait_all(reductions[0][0])
-    early = start_second(0)
-    total = jnp.zeros((2 * C, 4 * C), F32)
+    copies = exchange(3, ghid.at[pl.ds(1, 8)], 1024, LANE, sides_f.at[1])
+
+    first_a, second_a, third_a, finish_a = reduction(
+        grads_a, first_in_a, chunk_a, second_in_a, sums_a, 0
+    )
+    first_b, second_b, third_b, finish_b = reduction(
+        grads_b, first_in_b, chunk_b, second_in_b, sums_b, 1
+    )
+    kernel_terms(gcoarse_own, low3, term_c, 4, 512, LANE)
+    total_u = jnp.zeros((4 * C, 2 * C), F32)
+    total_d = jnp.zeros((2 * C, 4 * C), F32)
     for wz in range(4):
-        total = total + dot_t(gdown2[wz], quarters(act, wz))
-    grads[1, 12 * C : 14 * C, :] = total[:, 0:LANE].astype(BF16)
-    grads[1, 14 * C : 16 * C, 0:64] = total[:, LANE:192].astype(BF16)
-    kernel_terms(ghid, fine3, term_f, 8, 1024)
-    put_rows(1, term_f)
-    start_all(reductions[1][0])
+        total_u = total_u + dot_t(quarters(cot, wz), rect2[wz])
+        total_d = total_d + dot_t(gdown2[wz], quarters(act, wz))
+    put_rows(grads_b, term_c)
+    grads_b[512:704, 0 : 2 * C] = total_u.astype(BF16)
+    grads_b[704:800, :] = total_d[:, 0:LANE].astype(BF16)
+    grads_b[800:896, 0:64] = total_d[:, LANE:192].astype(BF16)
+    first_b()
+    kernel_terms(ghid, fine3, term_f, 8, 1024, 0)
+    put_rows(grads_a, term_f)
+    first_a()
+
+    for wz in range(4):
+        upward = dot(uup[...], rect2[wz])
+        for a in range(2):
+            for b in range(2):
+                k = 2 * a + b
+                for wx in range(4):
+                    lanes = pl.ds((2 * wx + b) * LANE, LANE)
+                    piece = upward[k * C : (k + 1) * C, wx * LANE : (wx + 1) * LANE]
+                    result[2 * wz + a, :, lanes] = (
+                        hidden[2 * wz + a + 1, :, lanes] + piece
+                    ).astype(BF16)
+    to_blocks(result, places, blocks_out)
+    own_b = second_b()
+    own_a = second_a()
 
     for copy in copies:
         copy.wait()
     widen(ghid.at[pl.ds(1, 8)], sides_f.at[1], edges_in.at[3], shift_f, ghid3, 8, 8, here)
     convolve(ghid3, wfb, hidden, 8, 1024)
-
-    wait_all(reductions[1][0])
-    late = start_second(1)
-    wait_all(reductions[0][1])
-    start_third(0, early)
-
     for z in range(8):
         result[z] = hidden[z + 1].astype(BF16)
     to_blocks(result, places, blocks_ig)
 
-    wait_all(reductions[1][1])
-    start_third(1, late)
-    wait_all(reductions[0][2])
-    wait_all(reductions[1][2])
-
-
-def unpack(sums, out_in, ig_in, out_hbm, ig_hbm, gf, gd, gc, gu, stage, sem):
+    third_b(own_b)
+    third_a(own_a)
+    finish_b()
+    finish_a()
+
+
+def unpack(sums_a, sums_b, out_in, ig_in, out_hbm, ig_hbm, gf, gd, gc, gu, stage, sem):
     copies = [
         pltpu.make_async_copy(out_in, out_hbm, sem.at[0]),
         pltpu.make_async_copy(ig_in, ig_hbm, sem.at[1]),
@@ -597,22 +713,24 @@
         copy.start()
     scale = 1.0 / math.sqrt(SLOTS * 512 * NX * NY)
 
-    for part, target in ((1, gf), (0, gc)):
+    for sums, target in ((sums_a, gf), (sums_b, gc)):
+        tail = sums[9 * C : 9 * C + 80, :]
+        tail = jnp.concatenate([tail[:, 0:64], tail[0:64, 64:LANE]], axis=0)
         rows = jnp.concatenate(
-            [sums[part, 3 * C * k : 3 * C * (k + 1), :] for k in range(4)], axis=1
+            [sums[3 * C * k : 3 * C * (k + 1), :] for k in range(3)] + [tail], axis=1
         )
         rows = rows.astype(F32) * scale
         for dz in range(3):
             for k in range(9):
                 block = rows[(2 - dz) * C : (3 - dz) * C, k * C : (k + 1) * C]
                 target[9 * dz + k] = block
-    tail = sums[1, 14 * C : 16 * C, :]
-    rows = jnp.concatenate([sums[1, 12 * C : 14 * C, :], tail, tail], axis=1)
+    tail = sums_b[800:896, :]
+    rows = jnp.concatenate([sums_b[704:800, :], tail, tail], axis=1)
     rows = rows.astype(F32) * scale
     for k in range(4):
         for e in range(2):
             gu[2 * k + e] = (
-                sums[0, (12 + k) * C : (13 + k) * C, e * C : (e + 1) * C].astype(F32) * scale
+                sums_b[512 + k * C : 512 + (k + 1) * C, e * C : (e + 1) * C].astype(F32) * scale
             )
             block = rows[e * C : (e + 1) * C, k * C : k * C + LANE]
             stage[pl.ds(2 * k + e, C, stride=8), :] = block
@@ -631,12 +749,18 @@
     blocks = (SLOTS, C, 512)
     kernel_shape = (27, C, C)
     block_shape = jax.ShapeDtypeStruct(blocks, BF16)
-    out, ig, sums = pl.pallas_call(
+    out, ig, sums_a, sums_b = pl.pallas_call(
         section,
-        out_shape=(block_shape, block_shape, jax.ShapeDtypeStruct((2, ROWS, LANE), BF16)),
-        in_specs=[smem, smem, vmem] + [hbm] * 5,
-        out_specs=(vmem, vmem, vmem),
+        out_shape=(
+            block_shape,
+            block_shape,
+            jax.ShapeDtypeStruct((ROWS_A, LANE), BF16),
+            jax.ShapeDtypeStruct((ROWS_B, LANE), BF16),
+        ),
+        in_specs=[smem, smem] + [hbm] * 6,
+        out_specs=(vmem, vmem, vmem, vmem),
         scratch_shapes=[
+            pltpu.VMEM(blocks, BF16),
             pltpu.VMEM(blocks, BF16),
             pltpu.VMEM(kernel_shape, BF16),
             pltpu.VMEM((C, 8, C), BF16),
@@ -656,7 +780,8 @@
             pltpu.VMEM((8, C, 1024), BF16),
             pltpu.VMEM((1024, 1024), BF16),
             pltpu.VMEM((8, 256, 256), BF16),
-            pltpu.VMEM((4, 256, 256), BF16),
+            pltpu.VMEM((4, 256, 384), BF16),
+            pltpu.VMEM((LANE, 256), BF16),
             pltpu.VMEM((1024, LANE), BF16),
             pltpu.VMEM((512, LANE), BF16),
             pltpu.VMEM((8, C, 1024), BF16),
@@ -665,10 +790,14 @@
             pltpu.VMEM((10, C, 1024), F32),
             pltpu.VMEM((8, C, 1024), BF16),
             pltpu.VMEM((4, C, 512), BF16),
-            pltpu.VMEM((4, 3 * C, 768), BF16),
+            pltpu.VMEM((4, 3 * C, 1024), BF16),
+            pltpu.VMEM((6, C, 768), F32),
             pltpu.VMEM((6, C, 512), F32),
             pltpu.VMEM((4, C, 512), F32),
+            pltpu.VMEM((4, C, 512), BF16),
+            pltpu.VMEM((4, C, 768), F32),
             pltpu.VMEM((4, 2 * C, 512), BF16),
+            pltpu.VMEM((4, C, 768), BF16),
             pltpu.VMEM((6, C, 512), BF16),
             pltpu.VMEM((4, 3 * C, 768), BF16),
             pltpu.VMEM((4, 2 * C, 512), BF16),
@@ -679,13 +808,18 @@
             pltpu.VMEM((3 * C, 9 * C), F32),
             pltpu.VMEM((4, C, LANE), BF16),
             pltpu.VMEM((2, 2, 8, C, LANE), BF16),
-            pltpu.VMEM((2, 2, 4, C, LANE), BF16),
+            pltpu.VMEM((2, 4, C, 2 * LANE), BF16),
+            pltpu.VMEM((2, 4, C, LANE), BF16),
             pltpu.VMEM((4, 6, C, LANE), BF16),
-            pltpu.VMEM((2, ROWS, LANE), BF16),
-            pltpu.VMEM((2, NY, CHUNK, LANE), BF16),
-            pltpu.VMEM((2, 2, CHUNK, LANE), BF16),
-            pltpu.VMEM((2, NX, CHUNK, LANE), BF16),
-            pltpu.SemaphoreType.DMA((5,)),
+            pltpu.VMEM((ROWS_A, LANE), BF16),
+            pltpu.VMEM((NY, ROWS_A // NY, LANE), BF16),
+            pltpu.VMEM((2, ROWS_A // NY, LANE), BF16),
+            pltpu.VMEM((NX, ROWS_A // NY, LANE), BF16),
+            pltpu.VMEM((ROWS_B, LANE), BF16),
+            pltpu.VMEM((NY, ROWS_B // NY, LANE), BF16),
+            pltpu.VMEM((2, ROWS_B // NY, LANE), BF16),
+            pltpu.VMEM((NX, ROWS_B // NY, LANE), BF16),
+            pltpu.SemaphoreType.DMA((6,)),
             pltpu.SemaphoreType.DMA((4, 8)),
             pltpu.SemaphoreType.DMA((4, 8)),
             pltpu.SemaphoreType.DMA((2, 3, NX)),
@@ -698,12 +832,17 @@
     )(
         block_slots.reshape(1, SLOTS),
         block_count.reshape(1, 1),
-        features.reshape(blocks),
-        cotangent.reshape(blocks),
-        fine_weight.transpose(1, 0, 2),
-        down_weight,
-        coarse_weight.transpose(1, 0, 2),
-        up_weight,
+        *(
+            pltpu.with_memory_space_constraint(value, pltpu.HBM)
+            for value in (
+                features.reshape(blocks),
+                cotangent.reshape(blocks),
+                fine_weight.transpose(1, 0, 2),
+                down_weight,
+                coarse_weight.transpose(1, 0, 2),
+                up_weight,
+            )
+        ),
     )
     out, ig, gf, gd, gc, gu = pl.pallas_call(
         unpack,
@@ -715,12 +854,12 @@
             jax.ShapeDtypeStruct(kernel_shape, F32),
             jax.ShapeDtypeStruct((8, C, C), F32),
         ),
-        in_specs=[vmem, vmem, vmem],
+        in_specs=[vmem, vmem, vmem, vmem],
         out_specs=(hbm, hbm, vmem, vmem, vmem, vmem),
         scratch_shapes=[pltpu.VMEM((8 * C, LANE), F32), pltpu.SemaphoreType.DMA((2,))],
         compiler_params=pltpu.CompilerParams(vmem_limit_bytes=8 * 1024 * 1024),
         name="unpack",
-    )(sums, out, ig)
+    )(sums_a, sums_b, out, ig)
     shape_out = (1, 1) + blocks
     gf, gc = gf.transpose(1, 0, 2), gc.transpose(1, 0, 2)
     return out.reshape(shape_out), ig.reshape(shape_out), gf, gd, gc, gu

time: 79.7 us -> 68.9 us (0.86)
  Pallas kernels: 72.4 us -> 66.6 us
  local copies, waits for them, and re-layouts: 5.51 us -> 0.65 us
    pallas_call x1, Pallas kernels: 69.7 us -> 64 us  [on_device(): pl.pallas_call(section, out_shape=(block_shape, block_shape, jax.ShapeDty...]
    unnamed x12 -> x2, local copies, waits for them, and re-layouts: 5.51 us -> 0.65 us
where the time goes in v4:
time: 68.9 us; the launch traced here: 68.7 us
  Pallas kernels  66.6 us (97%)
  between operations  1.46 us (2%)
    pallas_call x1, Pallas kernels, on_device(): pl.pallas_call(section, out_shape=(block_shape, block_shape, jax.ShapeDty...  64 us
    pallas_call x1, Pallas kernels, on_device(): pl.pallas_call(unpack, out_shape=(block_shape, block_shape, jax.ShapeDtyp...  2.67 us

profile of v4, /device:TPU:1, one launch (start us, length us, event | category | flops | bytes accessed | tf_op | source)
XLA Modules:
  0.0 68.7 jit_solution(4439950855029914403)
XLA Ops:
  1.3 0.0 copy-start
  1.3 0.6 copy-done
  1.9 64.0 %section.1 = (bf16[16,48,512]{2,1,0:T(8,128)(2,1)S(1)}, bf16[16,48,512]{2,1,0:T(8,128)(2,1)S(1)}, bf16[512,128]{1,0:T(8,128)(2,1)S(1)}, bf16[1024,128]{1,0:T(8,128)(2,1)S(1)}) custom-call(s32[1,16]{1,0:T(1,128)S(1)} %bitcast.9, s32[1,1]{1,0:T(1,128)S(6)} %copy.14.count_ref, bf16[16,48,512]{2,1,0:T(8,128)(2,1)} %bitcast.10, bf16[16,48,512]{2,1,0:T(8,128)(2,1)} %bitcast.11, ...), custom_call_target="tpu_custom_call" | custom-call | tf_op jit(solution)/shard_map/section/pallas_call | solution.py:752
  65.9 2.7 %unpack.1 = (bf16[16,48,512]{2,1,0:T(8,128)(2,1)}, bf16[16,48,512]{2,1,0:T(8,128)(2,1)}, f32[27,48,48]{2,1,0:T(8,128)}, f32[48,8,48]{2,1,0:T(8,128)}, f32[27,48,48]{2,1,0:T(8,128)}, /*index=5*/f32[8,48,48]{2,1,0:T(8,128)}) custom-call(bf16[512,128]{1,0:T(8,128)(2,1)S(1)} %get-tuple-element.16.sums_a, bf16[1024,128]{1,0:T(8,128)(2,1)S(1)} %get-tuple-element.17.sums_b, ...), custom_call_target="tpu_custom_call" | custom-call | tf_op jit(solution)/shard_map/unpack/pallas_call | solution.py:847
Async XLA Ops:
  1.3 0.7 copy-start

commit v5 on v4

--- a/solution.py
+++ b/solution.py
@@ -13,7 +13,7 @@
 NX = 16
 NY = 16
 ROWS_A = 512
-ROWS_B = 1024
+ROWS_B = 768
 F32 = jnp.float32
 BF16 = jnp.bfloat16
 MESH = pl.DeviceIdType.MESH
@@ -562,8 +562,9 @@
     def put_rows(grads, term):
         for k in range(3):
             grads[3 * C * k : 3 * C * (k + 1), :] = term[:, k * LANE : (k + 1) * LANE].astype(BF16)
-        grads[9 * C : 9 * C + 80, 0:C] = term[0:80, 3 * LANE :].astype(BF16)
-        grads[9 * C : 9 * C + 64, 64 : 64 + C] = term[80:144, 3 * LANE :].astype(BF16)
+        tail = term[:, 3 * LANE :]
+        grads[9 * C : 9 * C + 72, 0:C] = tail[0:72].astype(BF16)
+        grads[9 * C : 9 * C + 72, C : 2 * C] = tail[72:144].astype(BF16)
 
     load_feat.wait()
     to_grid(feat, work, places, fine)
@@ -651,9 +652,6 @@
                         + piece * slope(hidden[2 * wz + a + 1, :, lanes])
                     ).astype(BF16)
 
-    pack_edges(ghid[1:9], 8, edge_f, packed.at[3])
-    copies = exchange(3, ghid.at[pl.ds(1, 8)], 1024, LANE, sides_f.at[1])
-
     first_a, second_a, third_a, finish_a = reduction(
         grads_a, first_in_a, chunk_a, second_in_a, sums_a, 0
     )
@@ -667,13 +665,22 @@
         total_u = total_u + dot_t(quarters(cot, wz), rect2[wz])
         total_d = total_d + dot_t(gdown2[wz], quarters(act, wz))
     put_rows(grads_b, term_c)
+    low_d = total_d[:, 0:LANE].astype(BF16)
+    high_d = total_d[:, LANE:192].astype(BF16)
     grads_b[512:704, 0 : 2 * C] = total_u.astype(BF16)
-    grads_b[704:800, :] = total_d[:, 0:LANE].astype(BF16)
-    grads_b[800:896, 0:64] = total_d[:, LANE:192].astype(BF16)
+    grads_b[512:608, 96:LANE] = high_d[:, 0:32]
+    grads_b[608:704, 96:LANE] = high_d[:, 32:64]
+    grads_b[704:768, :] = low_d[0:64]
+    grads_b[432:464, 96:LANE] = low_d[64:96, 0:32]
+    grads_b[464:496, 96:LANE] = low_d[64:96, 32:64]
+    grads_a[432:464, 96:LANE] = low_d[64:96, 64:96]
+    grads_a[464:496, 96:LANE] = low_d[64:96, 96:LANE]
     first_b()
     kernel_terms(ghid, fine3, term_f, 8, 1024, 0)
     put_rows(grads_a, term_f)
     first_a()
+    pack_edges(ghid[1:9], 8, edge_f, packed.at[3])
+    copies = exchange(3, ghid.at[pl.ds(1, 8)], 1024, LANE, sides_f.at[1])
 
     for wz in range(4):
         upward = dot(uup[...], rect2[wz])
@@ -704,38 +711,80 @@
     finish_a()
 
 
-def unpack(sums_a, sums_b, out_in, ig_in, out_hbm, ig_hbm, gf, gd, gc, gu, stage, sem):
+def unpack(
+    sums_a,
+    sums_b,
+    out_in,
+    ig_in,
+    out_hbm,
+    ig_hbm,
+    gf_hbm,
+    gd_hbm,
+    gc_hbm,
+    gu_hbm,
+    gf,
+    gd,
+    gc,
+    gu,
+    stage,
+    sem,
+):
     copies = [
-        pltpu.make_async_copy(out_in, out_hbm, sem.at[0]),
-        pltpu.make_async_copy(ig_in, ig_hbm, sem.at[1]),
+        pltpu.make_async_copy(source, target, sem.at[k])
+        for k, (source, target) in enumerate(
+            (
+                (gf, gf_hbm),
+                (gc, gc_hbm),
+                (gu, gu_hbm),
+                (gd, gd_hbm),
+                (out_in, out_hbm),
+                (ig_in, ig_hbm),
+            )
+        )
     ]
-    for copy in copies:
-        copy.start()
+    copies[4].start()
+    copies[5].start()
     scale = 1.0 / math.sqrt(SLOTS * 512 * NX * NY)
 
-    for sums, target in ((sums_a, gf), (sums_b, gc)):
-        tail = sums[9 * C : 9 * C + 80, :]
-        tail = jnp.concatenate([tail[:, 0:64], tail[0:64, 64:LANE]], axis=0)
+    for part, (sums, target) in enumerate(((sums_a, gf), (sums_b, gc))):
+        tail = sums[9 * C : 9 * C + 80, :].astype(F32)
+        tail = jnp.concatenate([tail[0:72, 0:C], tail[0:72, C : 2 * C]], axis=0)
         rows = jnp.concatenate(
-            [sums[3 * C * k : 3 * C * (k + 1), :] for k in range(3)] + [tail], axis=1
+            [sums[3 * C * k : 3 * C * (k + 1), :].astype(F32) for k in range(3)] + [tail], axis=1
         )
-        rows = rows.astype(F32) * scale
+        rows = rows * scale
         for dz in range(3):
             for k in range(9):
                 block = rows[(2 - dz) * C : (3 - dz) * C, k * C : (k + 1) * C]
                 target[9 * dz + k] = block
-    tail = sums_b[800:896, :]
-    rows = jnp.concatenate([sums_b[704:800, :], tail, tail], axis=1)
-    rows = rows.astype(F32) * scale
+        copies[part].start()
     for k in range(4):
         for e in range(2):
-            gu[2 * k + e] = (
-                sums_b[512 + k * C : 512 + (k + 1) * C, e * C : (e + 1) * C].astype(F32) * scale
+            block = sums_b[512 + k * C : 512 + (k + 1) * C, e * C : (e + 1) * C]
+            gu[2 * k + e] = block.astype(F32) * scale
+    copies[2].start()
+    last = jnp.concatenate(
+        [
+            sums[first : first + 32, 96:LANE].astype(F32)
+            for sums in (sums_b, sums_a)
+            for first in (432, 464)
+        ],
+        axis=1,
+    )
+    low = jnp.concatenate([sums_b[704:768, :].astype(F32), last], axis=0)
+    high = jnp.concatenate(
+        [sums_b[512:608, 96:LANE].astype(F32), sums_b[608:704, 96:LANE].astype(F32)], axis=1
+    )
+    rows = jnp.concatenate([low, high], axis=1) * scale
+    for k in range(4):
+        for e in range(2):
+            block = rows[e * C : (e + 1) * C, k * C : (k + 1) * C]
+            stage[pl.ds(2 * k + e, C, stride=8), :] = jnp.concatenate(
+                [block, jnp.zeros((C, LANE - C), F32)], axis=1
             )
-            block = rows[e * C : (e + 1) * C, k * C : k * C + LANE]
-            stage[pl.ds(2 * k + e, C, stride=8), :] = block
     for o in range(C):
         gd[o] = stage[8 * o : 8 * o + 8, 0:C]
+    copies[3].start()
     for copy in copies:
         copy.wait()
 
@@ -855,8 +904,15 @@
             jax.ShapeDtypeStruct((8, C, C), F32),
         ),
         in_specs=[vmem, vmem, vmem, vmem],
-        out_specs=(hbm, hbm, vmem, vmem, vmem, vmem),
-        scratch_shapes=[pltpu.VMEM((8 * C, LANE), F32), pltpu.SemaphoreType.DMA((2,))],
+        out_specs=(hbm,) * 6,
+        scratch_shapes=[
+            pltpu.VMEM(kernel_shape, F32),
+            pltpu.VMEM((C, 8, C), F32),
+            pltpu.VMEM(kernel_shape, F32),
+            pltpu.VMEM((8, C, C), F32),
+            pltpu.VMEM((8 * C, LANE), F32),
+            pltpu.SemaphoreType.DMA((6,)),
+        ],
         compiler_params=pltpu.CompilerParams(vmem_limit_bytes=8 * 1024 * 1024),
         name="unpack",
     )(sums_a, sums_b, out, ig)

time: 68.9 us -> 67.3 us (0.977)
  Pallas kernels: 66.6 us -> 65.1 us
    pallas_call x1, Pallas kernels: 64 us -> 62.9 us  [on_device(): pl.pallas_call(section, out_shape=(block_shape, block_shape, jax.ShapeDty...]
where the time goes in v5:
time: 67.3 us; the launch traced here: 67.2 us
  Pallas kernels  65.1 us (97%)
  between operations  1.46 us (2%)
    pallas_call x1, Pallas kernels, on_device(): pl.pallas_call(section, out_shape=(block_shape, block_shape, jax.ShapeDty...  62.9 us
    pallas_call x1, Pallas kernels, on_device(): pl.pallas_call(unpack, out_shape=(block_shape, block_shape, jax.ShapeDtyp...  2.24 us

profile of v5, /device:TPU:1, one launch (start us, length us, event | category | flops | bytes accessed | tf_op | source)
XLA Modules:
  0.0 67.2 jit_solution(4212715565295379398)
XLA Ops:
  1.3 0.0 copy-start
  1.3 0.6 copy-done
  1.9 62.9 %section.1 = (bf16[16,48,512]{2,1,0:T(8,128)(2,1)S(1)}, bf16[16,48,512]{2,1,0:T(8,128)(2,1)S(1)}, bf16[512,128]{1,0:T(8,128)(2,1)S(1)}, bf16[768,128]{1,0:T(8,128)(2,1)S(1)}) custom-call(s32[1,16]{1,0:T(1,128)S(1)} %bitcast.9, s32[1,1]{1,0:T(1,128)S(6)} %copy.14.count_ref, bf16[16,48,512]{2,1,0:T(8,128)(2,1)} %bitcast.10, bf16[16,48,512]{2,1,0:T(8,128)(2,1)} %bitcast.11, ...), custom_call_target="tpu_custom_call" | custom-call | tf_op jit(solution)/shard_map/section/pallas_call | solution.py:801
  64.8 2.2 %unpack.1 = (bf16[16,48,512]{2,1,0:T(8,128)(2,1)}, bf16[16,48,512]{2,1,0:T(8,128)(2,1)}, f32[27,48,48]{2,1,0:T(8,128)}, f32[48,8,48]{2,1,0:T(8,128)}, f32[27,48,48]{2,1,0:T(8,128)}, /*index=5*/f32[8,48,48]{2,1,0:T(8,128)}) custom-call(bf16[512,128]{1,0:T(8,128)(2,1)S(1)} %get-tuple-element.16.sums_a, bf16[768,128]{1,0:T(8,128)(2,1)S(1)} %get-tuple-element.17.sums_b, ...), custom_call_target="tpu_custom_call" | custom-call | tf_op jit(solution)/shard_map/unpack/pallas_call | solution.py:896
Async XLA Ops:
  1.3 0.7 copy-start

commit v6 on v5

--- a/solution.py
+++ b/solution.py
@@ -203,20 +203,20 @@
     gx = place[0]
     halos = coarse_halos(received, place)
     zero = jnp.zeros((4 * C, LANE), BF16)
+    halves = []
+    for side, inside in ((0, gx > 0), (1, gx < NX - 1)):
+        rows = jnp.where(inside, sides[side].reshape(4 * C, LANE), zero)
+        halves.append([rows, pltpu.roll(rows.astype(F32), 64, 1).astype(BF16)])
     for column in range(8):
         if column < 2:
-            lanes = slice(column * LANE, (column + 1) * LANE)
-            rows = jnp.where(gx > 0, sides[0, :, :, lanes].reshape(4 * C, LANE), zero)
-            halo, x = halos[0], column + 2
+            rows, halo, x = halves[0][column], halos[0], column + 2
         elif column < 6:
             x = column - 2
             rows = grid[:, :, x * LANE : (x + 1) * LANE].reshape(4 * C, LANE)
             halo = halos[1]
         else:
             x = column - 6
-            lanes = slice(x * LANE, (x + 1) * LANE)
-            rows = jnp.where(gx < NX - 1, sides[1, :, :, lanes].reshape(4 * C, LANE), zero)
-            halo = halos[2]
+            rows, halo = halves[1][x], halos[2]
         moved = dot(jnp.concatenate([rows, halo], axis=1), s_ref[x]).astype(BF16)
         for t in range(3):
             part = moved[:, t * LANE : (t + 1) * LANE].reshape(4, C, LANE)
@@ -388,6 +388,7 @@
     term_c,
     packed,
     sides_f,
+    outer,
     sides_c,
     sides_g,
     edges_in,
@@ -453,22 +454,9 @@
     half_live = jnp.where(iota((8, LANE), 1) < 64, live, 0.0)
     lower = jnp.where(iota((8, LANE), 1) < 64, 1.0, 0.0)
 
-    def exchange(step, source, length, width, sides):
+    def exchange(step, sources, sides):
         copies = []
-        for side in range(2):
-            first = length - width if side == 0 else 0
-            shift = 1 if side == 0 else NX - 1
-            copies.append(
-                pltpu.make_async_remote_copy(
-                    src_ref=source.at[:, :, pl.ds(first, width)],
-                    dst_ref=sides.at[side],
-                    send_sem=send_sem.at[step, side],
-                    recv_sem=recv_sem.at[step, side],
-                    device_id=(lax.rem(gx + shift, NX), gy),
-                    device_id_type=MESH,
-                )
-            )
-        for row in range(3):
+        for row in (0, 2, 1):
             for side in range(2):
                 copies.append(
                     pltpu.make_async_remote_copy(
@@ -483,9 +471,23 @@
                         device_id_type=MESH,
                     )
                 )
+        for side in range(2):
+            copies.append(
+                pltpu.make_async_remote_copy(
+                    src_ref=sources[side],
+                    dst_ref=sides.at[side],
+                    send_sem=send_sem.at[step, side],
+                    recv_sem=recv_sem.at[step, side],
+                    device_id=(lax.rem(gx + (1 if side == 0 else NX - 1), NX), gy),
+                    device_id_type=MESH,
+                )
+            )
         for copy in copies:
             copy.start()
         return copies
+
+    def outer_columns(source, length):
+        return [source.at[:, :, pl.ds(first, LANE)] for first in (length - LANE, 0)]
 
     def reduction(grads, first_in, chunk, second_in, sums, part):
         rows = chunk.shape[1]
@@ -570,7 +572,7 @@
     to_grid(feat, work, places, fine)
     pack_edges(fine[...], 8, edge_f, packed.at[0])
     pl.semaphore_wait(barrier, 2 * (NX - 1) + 4)
-    copies = exchange(0, fine, 1024, LANE, sides_f.at[0])
+    copies = exchange(0, outer_columns(fine, 1024), sides_f.at[0])
 
     for load in loads:
         load.wait()
@@ -586,7 +588,6 @@
         grect[wz] = value
         grect_low[wz] = value.astype(BF16)
     pack_edges(grect_low[...], 4, edge_c, packed.at[2])
-    grect_copies = exchange(2, grect_low, 512, LANE, sides_g)
     build_shift_fine(shift_f)
     build_roll(roll_c)
     kernel_rows(fine_w, stack, eye, wf, wfb)
@@ -597,6 +598,7 @@
 
     for copy in copies:
         copy.wait()
+    grect_copies = exchange(2, outer_columns(grect_low, 512), sides_g)
     widen(fine, sides_f.at[0], edges_in.at[0], shift_f, fine3, 8, 8, here)
     convolve(fine3, wf, hidden, 8, 1024)
 
@@ -608,10 +610,14 @@
 
     for wz in range(4):
         both = dot(ddn[...], quarters(act, wz))
-        low[wz] = ((both[:C] + roll_half(both[C:])) * lower_mask).astype(BF16)
+        value = (both[:C] + roll_half(both[C:])) * lower_mask
+        low[wz] = value.astype(BF16)
+        for side, first in ((0, 2 * LANE), (1, 0)):
+            second = pltpu.roll(value[:, first + LANE : first + 2 * LANE], 64, 1)
+            outer[side, wz] = (value[:, first : first + LANE] + second).astype(BF16)
 
     pack_edges(low[...], 4, edge_c, packed.at[1])
-    copies = exchange(1, low, 512, 2 * LANE, sides_c)
+    copies = exchange(1, [outer.at[0], outer.at[1]], sides_c)
     for copy in grect_copies:
         copy.wait()
     extend_grect(grect, sides_g, edges_in.at[2], shift_c, grect_wide, here)
@@ -680,7 +686,7 @@
     put_rows(grads_a, term_f)
     first_a()
     pack_edges(ghid[1:9], 8, edge_f, packed.at[3])
-    copies = exchange(3, ghid.at[pl.ds(1, 8)], 1024, LANE, sides_f.at[1])
+    copies = exchange(3, outer_columns(ghid.at[pl.ds(1, 8)], 1024), sides_f.at[1])
 
     for wz in range(4):
         upward = dot(uup[...], rect2[wz])
@@ -857,7 +863,8 @@
             pltpu.VMEM((3 * C, 9 * C), F32),
             pltpu.VMEM((4, C, LANE), BF16),
             pltpu.VMEM((2, 2, 8, C, LANE), BF16),
-            pltpu.VMEM((2, 4, C, 2 * LANE), BF16),
+            pltpu.VMEM((2, 4, C, LANE), BF16),
+            pltpu.VMEM((2, 4, C, LANE), BF16),
             pltpu.VMEM((2, 4, C, LANE), BF16),
             pltpu.VMEM((4, 6, C, LANE), BF16),
             pltpu.VMEM((ROWS_A, LANE), BF16),
@@ -879,7 +886,7 @@
         ),
         name="section",
     )(
-        block_slots.reshape(1, SLOTS),
+        pltpu.with_memory_space_constraint(block_slots.reshape(1, SLOTS), pltpu.HBM),
         block_count.reshape(1, 1),
         *(
             pltpu.with_memory_space_constraint(value, pltpu.HBM)

time: 67.3 us -> 64.8 us (0.963)
  Pallas kernels: 65.1 us -> 63.3 us
    pallas_call x1, Pallas kernels: 62.9 us -> 61 us  [on_device(): pl.pallas_call(section, out_shape=(block_shape, block_shape, jax.ShapeDty...]
where the time goes in v6:
time: 64.8 us; the launch traced here: 64.7 us
  Pallas kernels  63.3 us (98%)
  between operations  1.45 us (2%)
    pallas_call x1, Pallas kernels, on_device(): pl.pallas_call(section, out_shape=(block_shape, block_shape, jax.ShapeDty...  61 us
    pallas_call x1, Pallas kernels, on_device(): pl.pallas_call(unpack, out_shape=(block_shape, block_shape, jax.ShapeDtyp...  2.24 us

profile of v6, /device:TPU:1, one launch (start us, length us, event | category | flops | bytes accessed | tf_op | source)
XLA Modules:
  0.0 64.7 jit_solution(10771338933545568986)
XLA Ops:
  1.3 61.0 %section.1 = (bf16[16,48,512]{2,1,0:T(8,128)(2,1)S(1)}, bf16[16,48,512]{2,1,0:T(8,128)(2,1)S(1)}, bf16[512,128]{1,0:T(8,128)(2,1)S(1)}, bf16[768,128]{1,0:T(8,128)(2,1)S(1)}) custom-call(s32[1,16]{1,0:T(1,128)} %bitcast.13, s32[1,1]{1,0:T(1,128)S(6)} %copy.14.count_ref, bf16[16,48,512]{2,1,0:T(8,128)(2,1)} %bitcast.9, bf16[16,48,512]{2,1,0:T(8,128)(2,1)} %bitcast.10, ...), custom_call_target="tpu_custom_call" | custom-call | tf_op jit(solution)/shard_map/section/pallas_call | solution.py:807
  62.3 2.2 %unpack.1 = (bf16[16,48,512]{2,1,0:T(8,128)(2,1)}, bf16[16,48,512]{2,1,0:T(8,128)(2,1)}, f32[27,48,48]{2,1,0:T(8,128)}, f32[48,8,48]{2,1,0:T(8,128)}, f32[27,48,48]{2,1,0:T(8,128)}, /*index=5*/f32[8,48,48]{2,1,0:T(8,128)}) custom-call(bf16[512,128]{1,0:T(8,128)(2,1)S(1)} %get-tuple-element.16.sums_a, bf16[768,128]{1,0:T(8,128)(2,1)S(1)} %get-tuple-element.17.sums_b, ...), custom_call_target="tpu_custom_call" | custom-call | tf_op jit(solution)/shard_map/unpack/pallas_call | solution.py:903

commit v7 on v6

--- a/solution.py
+++ b/solution.py
@@ -117,7 +117,7 @@
     return lax.fori_loop(0, SLOTS, step, jnp.zeros((8, LANE), F32))
 
 
-def to_grid(blocks, work, e_ref, grid):
+def to_grid(blocks, work, e_ref, grid, after_outer=None):
     for t in range(8):
         lanes = slice(t * LANE, (t + 1) * LANE)
         for pair in range(4):
@@ -126,7 +126,9 @@
             work[2 * pair, :, lanes] = jnp.concatenate([one[:, :64], two[:, :64]], axis=1)
             work[2 * pair + 1, :, lanes] = jnp.concatenate([one[:, 64:], two[:, 64:]], axis=1)
 
-    for n in range(4):
+    for n in (0, 3, 1, 2):
+        if n == 1 and after_outer is not None:
+            after_outer()
         lanes = slice(n * 256, (n + 1) * 256)
         moved = dot(work[...].reshape(8 * C, 1024), e_ref[:, lanes])
         grid[:, :, lanes] = moved.astype(BF16).reshape(8, C, 256)
@@ -454,7 +456,7 @@
     half_live = jnp.where(iota((8, LANE), 1) < 64, live, 0.0)
     lower = jnp.where(iota((8, LANE), 1) < 64, 1.0, 0.0)
 
-    def exchange(step, sources, sides):
+    def exchange_edges(step):
         copies = []
         for row in (0, 2, 1):
             for side in range(2):
@@ -471,6 +473,12 @@
                         device_id_type=MESH,
                     )
                 )
+        for copy in copies:
+            copy.start()
+        return copies
+
+    def exchange_sides(step, sources, sides):
+        copies = []
         for side in range(2):
             copies.append(
                 pltpu.make_async_remote_copy(
@@ -489,7 +497,7 @@
     def outer_columns(source, length):
         return [source.at[:, :, pl.ds(first, LANE)] for first in (length - LANE, 0)]
 
-    def reduction(grads, first_in, chunk, second_in, sums, part):
+    def reduction(grads, first_in, chunk, second_in, sums, part, steps):
         rows = chunk.shape[1]
 
         def chunk_rows(index):
@@ -516,6 +524,27 @@
                 device_id_type=MESH,
             )
 
+        def second_x(d):
+            x = lax.rem(gx, 4)
+            return pltpu.make_async_remote_copy(
+                src_ref=chunk.at[0],
+                dst_ref=second_in.at[d],
+                send_sem=sum_send.at[part, 1, d],
+                recv_sem=sum_recv.at[part, 1, d],
+                device_id=(gx - x + lax.rem(x + d, 4), gy),
+                device_id_type=MESH,
+            )
+
+        def second_z(d):
+            return pltpu.make_async_remote_copy(
+                src_ref=chunk.at[2],
+                dst_ref=second_in.at[4 + d],
+                send_sem=sum_send.at[part, 1, 4 + d],
+                recv_sem=sum_recv.at[part, 1, 4 + d],
+                device_id=(lax.rem(gx + 4 * d, NX), gy),
+                device_id_type=MESH,
+            )
+
         def third(d):
             return pltpu.make_async_remote_copy(
                 src_ref=chunk.at[1],
@@ -535,12 +564,28 @@
             for d in range(1, NY):
                 own = own + first_in[d].astype(F32)
             chunk[0] = own.astype(BF16)
-            start_all(second)
+            if steps == 1:
+                start_all(second)
+            else:
+                start_all(second_x, 4)
             return own
 
+        def start_middle(own):
+            wait_all(second_x, 4)
+            for d in range(1, 4):
+                own = own + second_in[d].astype(F32)
+            chunk[2] = own.astype(BF16)
+            start_all(second_z, 4)
+            return own
+
         def start_third(own):
-            wait_all(second)
-            for d in range(1, NX):
+            if steps == 1:
+                wait_all(second)
+                received = range(1, NX)
+            else:
+                wait_all(second_z, 4)
+                received = range(5, 8)
+            for d in received:
                 own = own + second_in[d].astype(F32)
             chunk[1] = own.astype(BF16)
             start_all(third)
@@ -549,15 +594,15 @@
         def finish():
             wait_all(third)
 
-        return start_first, start_second, start_third, finish
-
-    def start_all(copy):
-        @pl.loop(1, NX)
+        return start_first, start_second, start_middle, start_third, finish
+
+    def start_all(copy, count=NX):
+        @pl.loop(1, count)
         def _(d):
             copy(d).start()
 
-    def wait_all(copy):
-        @pl.loop(1, NX)
+    def wait_all(copy, count=NX):
+        @pl.loop(1, count)
         def _(d):
             copy(d).wait()
 
@@ -569,10 +614,15 @@
         grads[9 * C : 9 * C + 72, C : 2 * C] = tail[72:144].astype(BF16)
 
     load_feat.wait()
-    to_grid(feat, work, places, fine)
+    copies = []
+
+    def send_sides():
+        pl.semaphore_wait(barrier, 2 * (NX - 1) + 4)
+        copies.extend(exchange_sides(0, outer_columns(fine, 1024), sides_f.at[0]))
+
+    to_grid(feat, work, places, fine, send_sides)
     pack_edges(fine[...], 8, edge_f, packed.at[0])
-    pl.semaphore_wait(barrier, 2 * (NX - 1) + 4)
-    copies = exchange(0, outer_columns(fine, 1024), sides_f.at[0])
+    copies = copies + exchange_edges(0)
 
     for load in loads:
         load.wait()
@@ -589,16 +639,11 @@
         grect_low[wz] = value.astype(BF16)
     pack_edges(grect_low[...], 4, edge_c, packed.at[2])
     build_shift_fine(shift_f)
-    build_roll(roll_c)
     kernel_rows(fine_w, stack, eye, wf, wfb)
-    kernel_rows(coarse_w, stack, eye, wc, wcb)
-    grads_a[...] = jnp.zeros_like(grads_a)
-    grads_b[...] = jnp.zeros_like(grads_b)
-    gcoarse_own[...] = jnp.zeros_like(gcoarse_own)
 
     for copy in copies:
         copy.wait()
-    grect_copies = exchange(2, outer_columns(grect_low, 512), sides_g)
+    grect_copies = exchange_edges(2) + exchange_sides(2, outer_columns(grect_low, 512), sides_g)
     widen(fine, sides_f.at[0], edges_in.at[0], shift_f, fine3, 8, 8, here)
     convolve(fine3, wf, hidden, 8, 1024)
 
@@ -616,8 +661,14 @@
             second = pltpu.roll(value[:, first + LANE : first + 2 * LANE], 64, 1)
             outer[side, wz] = (value[:, first : first + LANE] + second).astype(BF16)
 
+    copies = exchange_sides(1, [outer.at[0], outer.at[1]], sides_c)
     pack_edges(low[...], 4, edge_c, packed.at[1])
-    copies = exchange(1, [outer.at[0], outer.at[1]], sides_c)
+    copies = copies + exchange_edges(1)
+    build_roll(roll_c)
+    kernel_rows(coarse_w, stack, eye, wc, wcb)
+    grads_a[...] = jnp.zeros_like(grads_a)
+    grads_b[...] = jnp.zeros_like(grads_b)
+    gcoarse_own[...] = jnp.zeros_like(gcoarse_own)
     for copy in grect_copies:
         copy.wait()
     extend_grect(grect, sides_g, edges_in.at[2], shift_c, grect_wide, here)
@@ -658,11 +709,11 @@
                         + piece * slope(hidden[2 * wz + a + 1, :, lanes])
                     ).astype(BF16)
 
-    first_a, second_a, third_a, finish_a = reduction(
-        grads_a, first_in_a, chunk_a, second_in_a, sums_a, 0
+    first_a, second_a, _, third_a, finish_a = reduction(
+        grads_a, first_in_a, chunk_a, second_in_a, sums_a, 0, 1
     )
-    first_b, second_b, third_b, finish_b = reduction(
-        grads_b, first_in_b, chunk_b, second_in_b, sums_b, 1
+    first_b, second_b, middle_b, third_b, finish_b = reduction(
+        grads_b, first_in_b, chunk_b, second_in_b, sums_b, 1, 2
     )
     kernel_terms(gcoarse_own, low3, term_c, 4, 512, LANE)
     total_u = jnp.zeros((4 * C, 2 * C), F32)
@@ -686,7 +737,8 @@
     put_rows(grads_a, term_f)
     first_a()
     pack_edges(ghid[1:9], 8, edge_f, packed.at[3])
-    copies = exchange(3, outer_columns(ghid.at[pl.ds(1, 8)], 1024), sides_f.at[1])
+    copies = exchange_edges(3)
+    copies = copies + exchange_sides(3, outer_columns(ghid.at[pl.ds(1, 8)], 1024), sides_f.at[1])
 
     for wz in range(4):
         upward = dot(uup[...], rect2[wz])
@@ -702,6 +754,7 @@
     to_blocks(result, places, blocks_out)
     own_b = second_b()
     own_a = second_a()
+    own_b = middle_b(own_b)
 
     for copy in copies:
         copy.wait()
@@ -873,7 +926,7 @@
             pltpu.VMEM((NX, ROWS_A // NY, LANE), BF16),
             pltpu.VMEM((ROWS_B, LANE), BF16),
             pltpu.VMEM((NY, ROWS_B // NY, LANE), BF16),
-            pltpu.VMEM((2, ROWS_B // NY, LANE), BF16),
+            pltpu.VMEM((3, ROWS_B // NY, LANE), BF16),
             pltpu.VMEM((NX, ROWS_B // NY, LANE), BF16),
             pltpu.SemaphoreType.DMA((6,)),
             pltpu.SemaphoreType.DMA((4, 8)),

time: 64.8 us -> 63 us (0.972)
  Pallas kernels: 63.3 us -> 61.5 us
    pallas_call x1, Pallas kernels: 61 us -> 59.2 us  [on_device(): pl.pallas_call(section, out_shape=(block_shape, block_shape, jax.ShapeDty...]
where the time goes in v7:
time: 63 us; the launch traced here: 62.9 us
  Pallas kernels  61.5 us (98%)
  between operations  1.45 us (2%)
    pallas_call x1, Pallas kernels, on_device(): pl.pallas_call(section, out_shape=(block_shape, block_shape, jax.ShapeDty...  59.2 us
    pallas_call x1, Pallas kernels, on_device(): pl.pallas_call(unpack, out_shape=(block_shape, block_shape, jax.ShapeDtyp...  2.24 us

profile of v7, /device:TPU:1, one launch (start us, length us, event | category | flops | bytes accessed | tf_op | source)
XLA Modules:
  0.0 62.9 jit_solution(15045968175541323952)
XLA Ops:
  1.3 59.2 %section.1 = (bf16[16,48,512]{2,1,0:T(8,128)(2,1)S(1)}, bf16[16,48,512]{2,1,0:T(8,128)(2,1)S(1)}, bf16[512,128]{1,0:T(8,128)(2,1)S(1)}, bf16[768,128]{1,0:T(8,128)(2,1)S(1)}) custom-call(s32[1,16]{1,0:T(1,128)} %bitcast.13, s32[1,1]{1,0:T(1,128)S(6)} %copy.14.count_ref, bf16[16,48,512]{2,1,0:T(8,128)(2,1)} %bitcast.9, bf16[16,48,512]{2,1,0:T(8,128)(2,1)} %bitcast.10, ...), custom_call_target="tpu_custom_call" | custom-call | tf_op jit(solution)/shard_map/section/pallas_call | solution.py:860
  60.5 2.2 %unpack.1 = (bf16[16,48,512]{2,1,0:T(8,128)(2,1)}, bf16[16,48,512]{2,1,0:T(8,128)(2,1)}, f32[27,48,48]{2,1,0:T(8,128)}, f32[48,8,48]{2,1,0:T(8,128)}, f32[27,48,48]{2,1,0:T(8,128)}, /*index=5*/f32[8,48,48]{2,1,0:T(8,128)}) custom-call(bf16[512,128]{1,0:T(8,128)(2,1)S(1)} %get-tuple-element.16.sums_a, bf16[768,128]{1,0:T(8,128)(2,1)S(1)} %get-tuple-element.17.sums_b, ...), custom_call_target="tpu_custom_call" | custom-call | tf_op jit(solution)/shard_map/unpack/pallas_call | solution.py:956

commit v8 on v7

--- a/solution.py
+++ b/solution.py
@@ -261,7 +261,6 @@
 
 
 def convolve(wide, weight, total, depth, width):
-    total[...] = jnp.zeros_like(total)
     for z in range(depth):
         for first in range(0, width, 256):
             piece = dot(weight[...], window(wide, z, first, 256)).reshape(3, C, 256)
@@ -431,8 +430,7 @@
 
     barrier = pltpu.get_barrier_semaphore()
 
-    @pl.loop(1, NX)
-    def _(d):
+    for d in (8, 7, 9, 6, 10, 5, 11, 4, 12, 3, 13, 2, 14, 1, 15):
         pl.semaphore_signal(
             barrier, inc=1, device_id=(lax.rem(gx + d, NX), gy), device_id_type=MESH
         )
@@ -555,56 +553,53 @@
                 device_id_type=MESH,
             )
 
+        flying = {}
+
         def start_first():
-            start_all(first)
+            flying["first"] = start_all(first)
 
         def start_second():
-            wait_all(first)
+            wait_all(flying["first"])
             own = grads[chunk_rows(gy), :].astype(F32)
             for d in range(1, NY):
                 own = own + first_in[d].astype(F32)
             chunk[0] = own.astype(BF16)
-            if steps == 1:
-                start_all(second)
-            else:
-                start_all(second_x, 4)
+            flying["second"] = start_all(second) if steps == 1 else start_all(second_x, 4)
             return own
 
         def start_middle(own):
-            wait_all(second_x, 4)
+            wait_all(flying["second"])
             for d in range(1, 4):
                 own = own + second_in[d].astype(F32)
             chunk[2] = own.astype(BF16)
-            start_all(second_z, 4)
+            flying["second"] = start_all(second_z, 4)
             return own
 
         def start_third(own):
-            if steps == 1:
-                wait_all(second)
-                received = range(1, NX)
-            else:
-                wait_all(second_z, 4)
-                received = range(5, 8)
-            for d in received:
+            wait_all(flying["second"])
+            for d in range(1, NX) if steps == 1 else range(5, 8):
                 own = own + second_in[d].astype(F32)
             chunk[1] = own.astype(BF16)
-            start_all(third)
+            flying["third"] = start_all(third)
             sums[chunk_rows(gy), :] = chunk[1]
 
         def finish():
-            wait_all(third)
+            wait_all(flying["third"])
 
         return start_first, start_second, start_middle, start_third, finish
 
+    sent = []
+
     def start_all(copy, count=NX):
-        @pl.loop(1, count)
-        def _(d):
-            copy(d).start()
-
-    def wait_all(copy, count=NX):
-        @pl.loop(1, count)
-        def _(d):
-            copy(d).wait()
+        started = [copy(d) for d in range(1, count)]
+        for one in started:
+            one.start()
+        sent.extend(started)
+        return started
+
+    def wait_all(started):
+        for one in started:
+            one.wait_recv()
 
     def put_rows(grads, term):
         for k in range(3):
@@ -640,6 +635,7 @@
     pack_edges(grect_low[...], 4, edge_c, packed.at[2])
     build_shift_fine(shift_f)
     kernel_rows(fine_w, stack, eye, wf, wfb)
+    hidden[...] = jnp.zeros_like(hidden)
 
     for copy in copies:
         copy.wait()
@@ -669,6 +665,10 @@
     grads_a[...] = jnp.zeros_like(grads_a)
     grads_b[...] = jnp.zeros_like(grads_b)
     gcoarse_own[...] = jnp.zeros_like(gcoarse_own)
+    coarse[...] = jnp.zeros_like(coarse)
+    ghid[0] = jnp.zeros((C, 1024), BF16)
+    ghid[9] = jnp.zeros((C, 1024), BF16)
+    coarse2[...] = jnp.zeros_like(coarse2)
     for copy in grect_copies:
         copy.wait()
     extend_grect(grect, sides_g, edges_in.at[2], shift_c, grect_wide, here)
@@ -691,8 +691,6 @@
     convolve(gcoarse3, wcb, coarse2, 4, 512)
 
     live_coarse = tile_lanes(half_live, C, 512)
-    ghid[0] = jnp.zeros((C, 1024), BF16)
-    ghid[9] = jnp.zeros((C, 1024), BF16)
     for wz in range(4):
         value = coarse2[wz + 1] * live_coarse
         gdown2[wz, 0:C] = value.astype(BF16)
@@ -752,6 +750,7 @@
                         hidden[2 * wz + a + 1, :, lanes] + piece
                     ).astype(BF16)
     to_blocks(result, places, blocks_out)
+    hidden[...] = jnp.zeros_like(hidden)
     own_b = second_b()
     own_a = second_a()
     own_b = middle_b(own_b)
@@ -768,6 +767,8 @@
     third_a(own_a)
     finish_b()
     finish_a()
+    for one in sent:
+        one.wait_send()
 
 
 def unpack(

time: 63 us -> 62.8 us (level)
  no operation moved by 1% of the time
where the time goes in v8:
time: 62.8 us; the launch traced here: 62.6 us
  Pallas kernels  61.2 us (97%)
  between operations  1.45 us (2%)
    pallas_call x1, Pallas kernels, on_device(): pl.pallas_call(section, out_shape=(block_shape, block_shape, jax.ShapeDty...  59 us
    pallas_call x1, Pallas kernels, on_device(): pl.pallas_call(unpack, out_shape=(block_shape, block_shape, jax.ShapeDtyp...  2.24 us

profile of v8, /device:TPU:1, one launch (start us, length us, event | category | flops | bytes accessed | tf_op | source)
XLA Modules:
  0.0 62.6 jit_solution(15151404901923195731)
XLA Ops:
  1.3 59.0 %section.1 = (bf16[16,48,512]{2,1,0:T(8,128)(2,1)S(1)}, bf16[16,48,512]{2,1,0:T(8,128)(2,1)S(1)}, bf16[512,128]{1,0:T(8,128)(2,1)S(1)}, bf16[768,128]{1,0:T(8,128)(2,1)S(1)}) custom-call(s32[1,16]{1,0:T(1,128)} %bitcast.13, s32[1,1]{1,0:T(1,128)S(6)} %copy.14.count_ref, bf16[16,48,512]{2,1,0:T(8,128)(2,1)} %bitcast.9, bf16[16,48,512]{2,1,0:T(8,128)(2,1)} %bitcast.10, ...), custom_call_target="tpu_custom_call" | custom-call | tf_op jit(solution)/shard_map/section/pallas_call | solution.py:861
  60.2 2.2 %unpack.1 = (bf16[16,48,512]{2,1,0:T(8,128)(2,1)}, bf16[16,48,512]{2,1,0:T(8,128)(2,1)}, f32[27,48,48]{2,1,0:T(8,128)}, f32[48,8,48]{2,1,0:T(8,128)}, f32[27,48,48]{2,1,0:T(8,128)}, /*index=5*/f32[8,48,48]{2,1,0:T(8,128)}) custom-call(bf16[512,128]{1,0:T(8,128)(2,1)S(1)} %get-tuple-element.16.sums_a, bf16[768,128]{1,0:T(8,128)(2,1)S(1)} %get-tuple-element.17.sums_b, ...), custom_call_target="tpu_custom_call" | custom-call | tf_op jit(solution)/shard_map/unpack/pallas_call | solution.py:957
